TPU v7x, 128 devices: a whole 4x4x4 slice. The times are simulated.
128 devices in a mesh: segment: 4 (over x), dom: 32 (over y, z, core).
Axes of the slice: x: 4, y: 4, z: 4, core: 2. Of those that a mesh axis runs over, the one named last changes fastest.
Arguments:
- features: bfloat16 [4, 16384, 512], P(None, 'dom'), may hold values from -6 to 6
- send_rows: int32 [4, 32, 32, 128], P(None, 'dom'), may hold values from 0 to 511
- send_len: int32 [4, 32, 32], P(None, 'dom'), may hold values from 0 to 128, as said below
- tile_src: int32 [4, 128, 4], P(None, 'dom'), may hold values from 0 to 35
- tile_count: int32 [4, 128], P(None, 'dom'), may hold values from 1 to 4, as said below
- tile_val: bfloat16 [4, 128, 4, 128, 128], P(None, 'dom'), may hold values from -0.25 to 0.25
- w_self: bfloat16 [4, 512, 512], P('segment'), may hold values from -0.25 to 0.25
- w_neigh: bfloat16 [4, 512, 512], P('segment'), may hold values from -0.25 to 0.25
- gain: bfloat16 [4, 512], P('segment'), may hold values from 0.25 to 1.75
- bias: bfloat16 [4, 512], P('segment'), may hold values from -3 to 3
Outputs:
- acts: bfloat16 [4, 4, 16384, 512], P('segment', None, 'dom')
Inputs may be any that keep to these rules, and one draw needn't show every extreme that they name: `send_len`: A partition sends nothing to itself; in every span each partition sends a full block of 128 rows to one other partition. `tile_count`: in every span one partition has 4 live tiles in each of its blocks.
All inputs are finite; a program needn't handle non-finite values.
Results may differ from a plain program's by a relative error of at most 0.0065.
Values may be sent and summed in bfloat16 or wider, within the bound.
A program may use at most 64 MiB of HBM per device.

v0:
```python
import jax
import jax.numpy as jnp
from jax import lax
from jax.sharding import PartitionSpec as P

norm_eps = 1e-05


def passed_along(shard, axis, by):
    peers = lax.axis_size(axis)
    pairs = [(i, i + by) for i in range(peers) if 0 <= i + by < peers]
    return lax.ppermute(shard, axis, pairs)


def select_span(array_in, span_id):
    return lax.dynamic_index_in_dim(array_in, span_id, 0, keepdims=False)


def sage_layer(inputs, span_id, graph, w_one, w_two, gain_one, bias_one):
    rows_all, lens_all, src_all, count_all, vals_all = graph
    send_list = select_span(rows_all, span_id)[0]
    send_count = select_span(lens_all, span_id)[0]
    tile_index = select_span(src_all, span_id)
    tile_total = select_span(count_all, span_id)
    tile_vals = select_span(vals_all, span_id)
    peer_count, tile_rows = send_list.shape
    feat_width = inputs.shape[1]
    block_count, tile_depth = tile_index.shape
    picked = jnp.take(inputs, send_list.reshape(-1), axis=0).reshape(
        peer_count, tile_rows, feat_width
    )
    row_live = lax.broadcasted_iota(jnp.int32, (peer_count, tile_rows), 1) < send_count[:, None]
    outgoing = jnp.where(row_live[:, :, None], picked, jnp.zeros_like(picked))
    incoming = lax.all_to_all(outgoing, "dom", split_axis=0, concat_axis=0, tiled=True)
    sources = jnp.concatenate(
        [inputs.reshape(block_count, tile_rows, feat_width), incoming], axis=0
    )
    tile_live = lax.broadcasted_iota(jnp.int32, (block_count, tile_depth), 1) < tile_total[:, None]

    def block_sum(packed):
        block_index, block_vals, block_live = packed
        chosen = jnp.take(sources, block_index, axis=0)
        masked = jnp.where(block_live[:, None, None], block_vals, jnp.zeros_like(block_vals))
        return jnp.einsum("kij,kjd->id", masked, chosen, preferred_element_type=jnp.float32)

    summed = lax.map(block_sum, (tile_index, tile_vals, tile_live))
    gathered = summed.reshape(block_count * tile_rows, feat_width).astype(jnp.bfloat16)
    mixed = jnp.dot(inputs, w_one, preferred_element_type=jnp.float32) + jnp.dot(
        gathered, w_two, preferred_element_type=jnp.float32
    )
    center = mixed - jnp.mean(mixed, axis=1, keepdims=True)
    spread = jnp.mean(center * center, axis=1, keepdims=True)
    scaled = center * lax.rsqrt(spread + norm_eps) * gain_one.astype(jnp.float32) + bias_one.astype(
        jnp.float32
    )
    return jnp.maximum(scaled, 0.0).astype(jnp.bfloat16)


def per_device(
    features, send_rows, send_len, tile_src, tile_count, tile_val, w_self, w_neigh, gain, bias
):
    segments = lax.axis_size("segment")
    segment_id = lax.axis_index("segment")
    span_total, node_rows, feat_width = features.shape
    graph = (send_rows, send_len, tile_src, tile_count, tile_val)
    carried = jnp.zeros((node_rows, feat_width), jnp.bfloat16)
    results = jnp.zeros((span_total, node_rows, feat_width), jnp.bfloat16)
    moments = span_total + segments - 1
    for moment in range(moments):
        span_id = jnp.clip(moment - segment_id, 0, span_total - 1)
        entering = features[min(moment, span_total - 1)]
        inputs = jnp.where(segment_id == 0, entering, carried)
        output = sage_layer(inputs, span_id, graph, w_self[0], w_neigh[0], gain[0], bias[0])
        active = (moment - segment_id >= 0) & (moment - segment_id < span_total)
        earlier = select_span(results, span_id)
        results = lax.dynamic_update_index_in_dim(
            results, jnp.where(active, output, earlier), span_id, 0
        )
        if moment + 1 < moments:
            carried = passed_along(output, "segment", 1)
    return results[None]


def solution(mesh):
    in_specs = (
        P(None, "dom", None),
        P(None, "dom", None, None),
        P(None, "dom", None),
        P(None, "dom", None),
        P(None, "dom"),
        P(None, "dom", None, None, None),
        P("segment", None, None),
        P("segment", None, None),
        P("segment", None),
        P("segment", None),
    )
    out_specs = P("segment", None, "dom", None)
    return jax.shard_map(
        per_device, mesh=mesh, in_specs=in_specs, out_specs=out_specs, check_vma=False
    )
```

profile of v0, /device:TPU:6, one launch (start us, length us, event | category | flops | bytes accessed | tf_op | source)
XLA Modules:
  0.0 845.0 jit_solution(12987161370666887648)
XLA Ops:
  7.1 17.4 %gather_fusion.7 = bf16[4096,512]{1,0:T(8,128)(2,1)} fusion(bf16[512,512]{1,0:T(8,128)(2,1)S(1)} %bitcast.374, s32[4096]{0:T(1024)S(1)} %get-tuple-element.371), kind=kCustom, calls=%fused_computation.clone | custom fusion | bytes 8404992 | tf_op jit(solution)/shard_map/jit(_take)/gather | solution.py:29
  41.7 49.1 %all-to-all-done = bf16[32,128,512]{2,1,0:T(8,128)(2,1)} async-done(((bf16[32,128,512]{2,1,0:T(8,128)(2,1)}), bf16[32,128,512]{2,1,0:T(8,128)(2,1)}, u32[]{:S(2)}, u32[]{:S(2)}) %all-to-all-start) | async-done | bytes 4194336 | tf_op jit(solution)/shard_map/all_to_all | solution.py:34
  95.6 16.9 %while.70 = (s32[]{:T(128)}, bf16[4,128,512]{2,1,0:T(8,128)(2,1)S(1)}, pred[4,4]{1,0:T(4,128)(4,1)S(1)}, bf16[4,4,128,128]{3,2,1,0:T(8,128)(2,1)}, s32[4,4]{1,0:...) while((s32[]{:T(128)}, bf16[4,128,512]{2,1,0:T(8,128)(2,1)S(1)}, pred[4,4]{1,0:T(4,128)(4,1)S(1)}, ...), condition=%wide.region_1.4_spmd, body=%wide.region_0.3_spmd.sunk | while | flops 67437592 | bytes 1972385 | solution.py:46
  115.2 13.9 %collective-permute-done = bf16[512,512]{0,1:T(8,128)(2,1)} collective-permute-done((bf16[512,512]{0,1:T(8,128)(2,1)S(1)}, bf16[512,512]{0,1:T(8,128)(2,1)}, u32[]{:S(2)}, u32[]{:S(2)}) %collective-permute-start) | collective-permute-done | bytes 524320 | tf_op jit(solution)/shard_map/ppermute | solution.py:12
  130.4 17.4 %gather_fusion.8 = bf16[4096,512]{1,0:T(8,128)(2,1)} fusion(bf16[512,512]{1,0:T(8,128)(2,1)S(1)} %copy.39, s32[4096]{0:T(1024)S(1)} %get-tuple-element.370), kind=kCustom, calls=%fused_computation.2.clone | custom fusion | bytes 8404992 | tf_op jit(solution)/shard_map/jit(_take)/gather | solution.py:29
  161.3 50.7 %all-to-all-done.1 = bf16[32,128,512]{2,1,0:T(8,128)(2,1)} async-done(((bf16[32,128,512]{2,1,0:T(8,128)(2,1)}), bf16[32,128,512]{2,1,0:T(8,128)(2,1)}, u32[]{:S(2)}, u32[]{:S(2)}) %all-to-all-start.1) | async-done | bytes 4194336 | tf_op jit(solution)/shard_map/all_to_all | solution.py:34
  216.8 16.9 %while.71 = (s32[]{:T(128)}, bf16[4,128,512]{2,1,0:T(8,128)(2,1)S(1)}, pred[4,4]{1,0:T(4,128)(4,1)S(1)}, bf16[4,4,128,128]{3,2,1,0:T(8,128)(2,1)}, s32[4,4]{1,0:...) while((s32[]{:T(128)}, bf16[4,128,512]{2,1,0:T(8,128)(2,1)S(1)}, pred[4,4]{1,0:T(4,128)(4,1)S(1)}, ...), condition=%wide.region_5.8_spmd, body=%wide.region_4.7_spmd.sunk | while | flops 67437592 | bytes 1972385 | solution.py:46
  251.7 17.4 %gather_fusion.9 = bf16[4096,512]{1,0:T(8,128)(2,1)} fusion(bf16[512,512]{1,0:T(8,128)(2,1)S(1)} %copy.40, s32[4096]{0:T(1024)S(1)} %get-tuple-element.369), kind=kCustom, calls=%fused_computation.3.clone | custom fusion | bytes 8404992 | tf_op jit(solution)/shard_map/jit(_take)/gather | solution.py:29
  283.3 50.1 %all-to-all-done.2 = bf16[32,128,512]{2,1,0:T(8,128)(2,1)} async-done(((bf16[32,128,512]{2,1,0:T(8,128)(2,1)}), bf16[32,128,512]{2,1,0:T(8,128)(2,1)}, u32[]{:S(2)}, u32[]{:S(2)}) %all-to-all-start.2) | async-done | bytes 4194336 | tf_op jit(solution)/shard_map/all_to_all | solution.py:34
  338.2 16.9 %while.72 = (s32[]{:T(128)}, bf16[4,128,512]{2,1,0:T(8,128)(2,1)S(1)}, pred[4,4]{1,0:T(4,128)(4,1)S(1)}, bf16[4,4,128,128]{3,2,1,0:T(8,128)(2,1)}, s32[4,4]{1,0:...) while((s32[]{:T(128)}, bf16[4,128,512]{2,1,0:T(8,128)(2,1)S(1)}, pred[4,4]{1,0:T(4,128)(4,1)S(1)}, ...), condition=%wide.region_9.12_spmd, body=%wide.region_8.11_spmd.sunk | while | flops 67437592 | bytes 1972385 | solution.py:46
  373.1 17.4 %gather_fusion.10 = bf16[4096,512]{1,0:T(8,128)(2,1)} fusion(bf16[512,512]{1,0:T(8,128)(2,1)S(1)} %copy.41, s32[4096]{0:T(1024)S(1)} %get-tuple-element.368), kind=kCustom, calls=%fused_computation.4.clone | custom fusion | bytes 8404992 | tf_op jit(solution)/shard_map/jit(_take)/gather | solution.py:29
  406.3 48.5 %all-to-all-done.3 = bf16[32,128,512]{2,1,0:T(8,128)(2,1)} async-done(((bf16[32,128,512]{2,1,0:T(8,128)(2,1)}), bf16[32,128,512]{2,1,0:T(8,128)(2,1)}, u32[]{:S(2)}, u32[]{:S(2)}) %all-to-all-start.3) | async-done | bytes 4194336 | tf_op jit(solution)/shard_map/all_to_all | solution.py:34
  459.6 16.9 %while.73 = (s32[]{:T(128)}, bf16[4,128,512]{2,1,0:T(8,128)(2,1)S(1)}, pred[4,4]{1,0:T(4,128)(4,1)S(1)}, bf16[4,4,128,128]{3,2,1,0:T(8,128)(2,1)}, s32[4,4]{1,0:...) while((s32[]{:T(128)}, bf16[4,128,512]{2,1,0:T(8,128)(2,1)S(1)}, pred[4,4]{1,0:T(4,128)(4,1)S(1)}, ...), condition=%wide.region_13.16_spmd, body=%wide.region_12.15_spmd.sunk | while | flops 67437592 | bytes 1972385 | solution.py:46
  480.2 14.0 %collective-permute-done.3 = bf16[512,512]{0,1:T(8,128)(2,1)S(1)} collective-permute-done((bf16[512,512]{0,1:T(8,128)(2,1)S(1)}, bf16[512,512]{0,1:T(8,128)(2,1)S(1)}, u32[]{:S(2)}, u32[]{:S(2)}) %collective-permute-start.3) | collective-permute-done | bytes 524320 | tf_op jit(solution)/shard_map/ppermute | solution.py:12
  494.4 17.4 %gather_fusion.11 = bf16[4096,512]{1,0:T(8,128)(2,1)} fusion(bf16[512,512]{1,0:T(8,128)(2,1)S(1)} %copy.42, s32[4096]{0:T(1024)S(1)} %get-tuple-element.367), kind=kCustom, calls=%fused_computation.5.clone | custom fusion | bytes 8404992 | tf_op jit(solution)/shard_map/jit(_take)/gather | solution.py:29
  527.6 48.5 %all-to-all-done.4 = bf16[32,128,512]{2,1,0:T(8,128)(2,1)} async-done(((bf16[32,128,512]{2,1,0:T(8,128)(2,1)}), bf16[32,128,512]{2,1,0:T(8,128)(2,1)}, u32[]{:S(2)}, u32[]{:S(2)}) %all-to-all-start.4) | async-done | bytes 4194336 | tf_op jit(solution)/shard_map/all_to_all | solution.py:34
  580.9 16.9 %while.74 = (s32[]{:T(128)}, bf16[4,128,512]{2,1,0:T(8,128)(2,1)S(1)}, pred[4,4]{1,0:T(4,128)(4,1)S(1)}, bf16[4,4,128,128]{3,2,1,0:T(8,128)(2,1)}, s32[4,4]{1,0:...) while((s32[]{:T(128)}, bf16[4,128,512]{2,1,0:T(8,128)(2,1)S(1)}, pred[4,4]{1,0:T(4,128)(4,1)S(1)}, ...), condition=%wide.region_17.20_spmd, body=%wide.region_16.19_spmd.sunk | while | flops 67437592 | bytes 1972385 | solution.py:46
  615.8 17.4 %gather_fusion.12 = bf16[4096,512]{1,0:T(8,128)(2,1)} fusion(bf16[512,512]{1,0:T(8,128)(2,1)S(1)} %copy.43, s32[4096]{0:T(1024)S(1)} %get-tuple-element.372), kind=kCustom, calls=%fused_computation.6.clone | custom fusion | bytes 8404992 | tf_op jit(solution)/shard_map/jit(_take)/gather | solution.py:29
  649.0 48.5 %all-to-all-done.5 = bf16[32,128,512]{2,1,0:T(8,128)(2,1)} async-done(((bf16[32,128,512]{2,1,0:T(8,128)(2,1)}), bf16[32,128,512]{2,1,0:T(8,128)(2,1)}, u32[]{:S(2)}, u32[]{:S(2)}) %all-to-all-start.5) | async-done | bytes 4194336 | tf_op jit(solution)/shard_map/all_to_all | solution.py:34
  702.2 16.9 %while.75 = (s32[]{:T(128)}, bf16[4,128,512]{2,1,0:T(8,128)(2,1)S(1)}, pred[4,4]{1,0:T(4,128)(4,1)S(1)}, bf16[4,4,128,128]{3,2,1,0:T(8,128)(2,1)}, s32[4,4]{1,0:...) while((s32[]{:T(128)}, bf16[4,128,512]{2,1,0:T(8,128)(2,1)S(1)}, pred[4,4]{1,0:T(4,128)(4,1)S(1)}, ...), condition=%wide.region_21.24_spmd, body=%wide.region_20.23_spmd.sunk | while | flops 67437592 | bytes 1972385 | solution.py:46
  722.1 14.0 %collective-permute-done.5 = bf16[512,512]{0,1:T(8,128)(2,1)S(1)} collective-permute-done((bf16[512,512]{0,1:T(8,128)(2,1)S(1)}, bf16[512,512]{0,1:T(8,128)(2,1)S(1)}, u32[]{:S(2)}, u32[]{:S(2)}) %collective-permute-start.5) | collective-permute-done | bytes 524320 | tf_op jit(solution)/shard_map/ppermute | solution.py:12
  736.3 17.4 %gather_fusion.13 = bf16[4096,512]{1,0:T(8,128)(2,1)} fusion(bf16[512,512]{1,0:T(8,128)(2,1)S(1)} %copy.44, s32[4096]{0:T(1024)S(1)} %copy-done.11), kind=kCustom, calls=%fused_computation.7.clone | custom fusion | bytes 8404992 | tf_op jit(solution)/shard_map/jit(_take)/gather | solution.py:29
  767.8 50.3 %all-to-all-done.6 = bf16[32,128,512]{2,1,0:T(8,128)(2,1)} async-done(((bf16[32,128,512]{2,1,0:T(8,128)(2,1)}), bf16[32,128,512]{2,1,0:T(8,128)(2,1)}, u32[]{:S(2)}, u32[]{:S(2)}) %all-to-all-start.6) | async-done | bytes 4194336 | tf_op jit(solution)/shard_map/all_to_all | solution.py:34
  822.9 19.5 %while.76 = (s32[]{:T(128)}, bf16[4,128,512]{2,1,0:T(8,128)(2,1)S(1)}, pred[4,4]{1,0:T(4,128)(4,1)S(1)}, bf16[4,4,128,128]{3,2,1,0:T(8,128)(2,1)}, s32[4,4]{1,0:...) while((s32[]{:T(128)}, bf16[4,128,512]{2,1,0:T(8,128)(2,1)S(1)}, pred[4,4]{1,0:T(4,128)(4,1)S(1)}, ...), condition=%wide.region_25.28_spmd, body=%wide.region_24.27_spmd.sunk | while | flops 67437592 | bytes 1972385 | solution.py:46
  (331 shorter events, 333.6 us)
Async XLA Ops:
  0.0 41.2 %copy-start = (bf16[1,512,512]{2,1,0:T(8,128)(2,1)S(1)}, bf16[1,512,512]{2,1,0:T(8,128)(2,1)}, u32[]{:S(2)}) copy-start(bf16[1,512,512]{2,1,0:T(8,128)(2,1)} %param.34) | copy-start | bytes 1572868
  29.4 8.6 %copy-start.16 = (bf16[1,512]{1,0:T(2,128)(2,1)S(1)}, bf16[1,512]{1,0:T(2,128)(2,1)}, u32[]{:S(2)}) copy-start(bf16[1,512]{1,0:T(2,128)(2,1)} %param.36) | copy-start | bytes 3076
  29.4 8.7 %copy-start.17 = (bf16[1,512]{1,0:T(2,128)(2,1)S(1)}, bf16[1,512]{1,0:T(2,128)(2,1)}, u32[]{:S(2)}) copy-start(bf16[1,512]{1,0:T(2,128)(2,1)} %param.37) | copy-start | bytes 3076
  29.4 8.7 %copy-start.15 = (s32[4,4]{1,0:T(4,128)S(1)}, s32[4,4]{1,0:T(4,128)}, u32[]{:S(2)}) copy-start(s32[4,4]{1,0:T(4,128)} %param.32) | copy-start | bytes 196
  29.4 9.3 %copy-start.12 = (s32[4,4,4]{2,1,0:T(4,128)S(1)}, s32[4,4,4]{2,1,0:T(4,128)}, u32[]{:S(2)}) copy-start(s32[4,4,4]{2,1,0:T(4,128)} %param.31) | copy-start | bytes 772
  29.4 9.9 %copy-start.3 = (bf16[4,4,4,128,128]{4,3,2,1,0:T(8,128)(2,1)S(1)}, bf16[4,4,4,128,128]{4,3,2,1,0:T(8,128)(2,1)}, u32[]{:S(2)}) copy-start(bf16[4,4,4,128,128]{4,3,2,1,0:T(8,128)(2,1)} %param.33) | copy-start | bytes 6291460
  29.4 61.4 %all-to-all-start = ((bf16[32,128,512]{2,1,0:T(8,128)(2,1)}), bf16[32,128,512]{2,1,0:T(8,128)(2,1)}, u32[]{:S(2)}, u32[]{:S(2)}) async-start(bf16[32,128,512]{2,1,0:T(8,128)(2,1)} %broadcast_select_fusion.13), calls=%async_computation | async-start | bytes 8388608 | tf_op jit(solution)/shard_map/all_to_all | solution.py:34
  95.6 16.9 %copy-start.1 = (bf16[1,512,512]{2,1,0:T(8,128)(2,1)S(1)}, bf16[1,512,512]{2,1,0:T(8,128)(2,1)}, u32[]{:S(2)}) copy-start(bf16[1,512,512]{2,1,0:T(8,128)(2,1)} %param.35) | copy-start | bytes 1572868
  113.6 15.5 %collective-permute-start = (bf16[512,512]{0,1:T(8,128)(2,1)S(1)}, bf16[512,512]{0,1:T(8,128)(2,1)}, u32[]{:S(2)}, u32[]{:S(2)}) collective-permute-start(bf16[512,512]{0,1:T(8,128)(2,1)S(1)} %get-tuple-element.347), channel_id=1, source_target_pairs={{0,32},{32,64},{64,96},{1,33},{33,65},{65,97},{2,34},{34,66},{66,9... | collective-permute-start | bytes 1572872 | tf_op jit(solution)/shard_map/ppermute | solution.py:12
  152.6 59.4 %all-to-all-start.1 = ((bf16[32,128,512]{2,1,0:T(8,128)(2,1)}), bf16[32,128,512]{2,1,0:T(8,128)(2,1)}, u32[]{:S(2)}, u32[]{:S(2)}) async-start(bf16[32,128,512]{2,1,0:T(8,128)(2,1)} %broadcast_select_fusion.12), calls=%async_computation.1 | async-start | bytes 8388608 | tf_op jit(solution)/shard_map/all_to_all | solution.py:34
  236.1 15.3 %collective-permute-start.1 = (bf16[512,512]{0,1:T(8,128)(2,1)S(1)}, bf16[512,512]{0,1:T(8,128)(2,1)S(1)}, u32[]{:S(2)}, u32[]{:S(2)}) collective-permute-start(bf16[512,512]{0,1:T(8,128)(2,1)S(1)} %get-tuple-element.345), channel_id=1, source_target_pairs={{0,32},{32,64},{64,96},{1,33},{33,65},{65,97},{2,34},{34,66},{66,9... | collective-permute-start | bytes 1572872 | tf_op jit(solution)/shard_map/ppermute | solution.py:12
  274.0 7.0 copy-start.10
  274.0 59.5 %all-to-all-start.2 = ((bf16[32,128,512]{2,1,0:T(8,128)(2,1)}), bf16[32,128,512]{2,1,0:T(8,128)(2,1)}, u32[]{:S(2)}, u32[]{:S(2)}) async-start(bf16[32,128,512]{2,1,0:T(8,128)(2,1)} %broadcast_select_fusion.11), calls=%async_computation.2 | async-start | bytes 8388608 | tf_op jit(solution)/shard_map/all_to_all | solution.py:34
  357.5 15.4 %collective-permute-start.2 = (bf16[512,512]{0,1:T(8,128)(2,1)S(1)}, bf16[512,512]{0,1:T(8,128)(2,1)S(1)}, u32[]{:S(2)}, u32[]{:S(2)}) collective-permute-start(bf16[512,512]{0,1:T(8,128)(2,1)S(1)} %get-tuple-element.343), channel_id=1, source_target_pairs={{0,32},{32,64},{64,96},{1,33},{33,65},{65,97},{2,34},{34,66},{66,9... | collective-permute-start | bytes 1572872 | tf_op jit(solution)/shard_map/ppermute | solution.py:12
  395.4 59.4 %all-to-all-start.3 = ((bf16[32,128,512]{2,1,0:T(8,128)(2,1)}), bf16[32,128,512]{2,1,0:T(8,128)(2,1)}, u32[]{:S(2)}, u32[]{:S(2)}) async-start(bf16[32,128,512]{2,1,0:T(8,128)(2,1)} %broadcast_select_fusion.10), calls=%async_computation.3 | async-start | bytes 8388608 | tf_op jit(solution)/shard_map/all_to_all | solution.py:34
  478.8 15.4 %collective-permute-start.3 = (bf16[512,512]{0,1:T(8,128)(2,1)S(1)}, bf16[512,512]{0,1:T(8,128)(2,1)S(1)}, u32[]{:S(2)}, u32[]{:S(2)}) collective-permute-start(bf16[512,512]{0,1:T(8,128)(2,1)S(1)} %get-tuple-element.341), channel_id=1, source_target_pairs={{0,32},{32,64},{64,96},{1,33},{33,65},{65,97},{2,34},{34,66},{66,9... | collective-permute-start | bytes 1572872 | tf_op jit(solution)/shard_map/ppermute | solution.py:12
  516.7 59.4 %all-to-all-start.4 = ((bf16[32,128,512]{2,1,0:T(8,128)(2,1)}), bf16[32,128,512]{2,1,0:T(8,128)(2,1)}, u32[]{:S(2)}, u32[]{:S(2)}) async-start(bf16[32,128,512]{2,1,0:T(8,128)(2,1)} %broadcast_select_fusion.9), calls=%async_computation.4 | async-start | bytes 8388608 | tf_op jit(solution)/shard_map/all_to_all | solution.py:34
  600.1 15.3 %collective-permute-start.4 = (bf16[512,512]{0,1:T(8,128)(2,1)S(1)}, bf16[512,512]{0,1:T(8,128)(2,1)S(1)}, u32[]{:S(2)}, u32[]{:S(2)}) collective-permute-start(bf16[512,512]{0,1:T(8,128)(2,1)S(1)} %get-tuple-element.339), channel_id=1, source_target_pairs={{0,32},{32,64},{64,96},{1,33},{33,65},{65,97},{2,34},{34,66},{66,9... | collective-permute-start | bytes 1572872 | tf_op jit(solution)/shard_map/ppermute | solution.py:12
  615.8 17.4 %copy-start.14 = (pred[4096]{0:T(1024)(128)(4,1)S(1)}, pred[4096]{0:T(1024)(128)(4,1)}, u32[]{:S(2)}) copy-start(pred[4096]{0:T(1024)(128)(4,1)} %get-tuple-element.360) | copy-start | bytes 12292
  638.1 59.4 %all-to-all-start.5 = ((bf16[32,128,512]{2,1,0:T(8,128)(2,1)}), bf16[32,128,512]{2,1,0:T(8,128)(2,1)}, u32[]{:S(2)}, u32[]{:S(2)}) async-start(bf16[32,128,512]{2,1,0:T(8,128)(2,1)} %broadcast_select_fusion.8), calls=%async_computation.5 | async-start | bytes 8388608 | tf_op jit(solution)/shard_map/all_to_all | solution.py:34
  719.6 16.7 %copy-start.11 = (s32[4096]{0:T(1024)S(1)}, s32[4096]{0:T(1024)}, u32[]{:S(2)}) copy-start(s32[4096]{0:T(1024)} %get-tuple-element.366) | copy-start | bytes 49156
  720.7 15.3 %collective-permute-start.5 = (bf16[512,512]{0,1:T(8,128)(2,1)S(1)}, bf16[512,512]{0,1:T(8,128)(2,1)S(1)}, u32[]{:S(2)}, u32[]{:S(2)}) collective-permute-start(bf16[512,512]{0,1:T(8,128)(2,1)S(1)} %get-tuple-element.337), channel_id=1, source_target_pairs={{0,32},{32,64},{64,96},{1,33},{33,65},{65,97},{2,34},{34,66},{66,9... | collective-permute-start | bytes 1572872 | tf_op jit(solution)/shard_map/ppermute | solution.py:12
  736.3 17.4 %copy-start.13 = (pred[4096]{0:T(1024)(128)(4,1)S(1)}, pred[4096]{0:T(1024)(128)(4,1)}, u32[]{:S(2)}) copy-start(pred[4096]{0:T(1024)(128)(4,1)} %get-tuple-element.359) | copy-start | bytes 12292
  758.6 59.5 %all-to-all-start.6 = ((bf16[32,128,512]{2,1,0:T(8,128)(2,1)}), bf16[32,128,512]{2,1,0:T(8,128)(2,1)}, u32[]{:S(2)}, u32[]{:S(2)}) async-start(bf16[32,128,512]{2,1,0:T(8,128)(2,1)} %broadcast_select_fusion.7), calls=%async_computation.6 | async-start | bytes 8388608 | tf_op jit(solution)/shard_map/all_to_all | solution.py:34
  (9 other events, 24.2 us)
where the time goes:
time: 850 us; the launch traced here: 845 us
  waiting for transfers between devices  429 us (50%)
  local copies, waits for them, and re-layouts  231 us (27%)
  other arithmetic  85.7 us (10%)
  starting transfers between devices  56.6 us (7%)
  matrix products  41 us (5%)
    all_to_all x7, waiting for transfers between devices, sage_layer(): lax.all_to_all(outgoing, 'dom', split_axis=0, concat_axis=0, tiled=True)  346 us
    gather x7, local copies, waits for them, and re-layouts, sage_layer(): jnp.take(inputs, send_list.reshape(-1), axis=0)  122 us
    ppermute x6, waiting for transfers between devices, passed_along(): return lax.ppermute(shard, axis, pairs)  83.1 us
    gather x28, local copies, waits for them, and re-layouts, block_sum(): chosen = jnp.take(sources, block_index, axis=0)  81.7 us
    all_to_all x7, starting transfers between devices, sage_layer(): lax.all_to_all(outgoing, 'dom', split_axis=0, concat_axis=0, tiled=True)  48.7 us
    dot_general x28, matrix products, block_sum(): jnp.einsum('kij,kjd->id', masked, chosen, preferred_element_type=jnp.floa...  34.1 us
    concatenate x7, other arithmetic, sage_layer(): jnp.concatenate([inputs.reshape(block_count, tile_rows, feat_width), inco...  33.2 us
    select_n x7, other arithmetic, sage_layer(): jnp.take(inputs, send_list.reshape(-1), axis=0)  18.1 us
  transfers between devices with their start and end apart: 13, of which 13 were waited for; matrix products, arithmetic and copies ran while one was open for 3% of the time, Pallas kernels for 0%

commit v1 on v0

v1 whole, which is shorter than its diff:
```python
import jax
import jax.numpy as jnp
from jax import lax
from jax.experimental import pallas as pl
from jax.experimental.pallas import tpu as pltpu
from jax.sharding import PartitionSpec as P

norm_eps = 1e-05
MESH = pl.DeviceIdType.MESH
F32, BF16, I32 = jnp.float32, jnp.bfloat16, jnp.int32
LAYERS = 4
RING = 4
CHIPS = 16
TILE = 128
ROWS = 512
D = 512
FS = 32
AUX = 128


def kernel(
    feat_hbm, rows_ref, len_ref, src_ref, cnt_ref, tv_hbm, ws_ref, wn_ref, gain_ref, bias_ref,
    out_hbm,
    feat, xt, wp, tv, meta, m1a, px, m1b, m1c, xc, xf, aggs, agg, outr, pre, qs,
    loc_sem, tv_s, tv_r, t1_s, t1_r, fw_s, fw_r, t2_s, t2_r, w_s, w_r, o_s, o_r, m_s, m_r, mb_s, mb_r, pm_s, pm_r,
):
    x = lax.axis_index("segment")
    d = lax.axis_index("dom")
    k = lax.rem(d, 2)
    r = lax.div(d, 2)
    y, z = lax.div(r, RING), lax.rem(r, RING)

    def to(o):
        return lax.rem(y + lax.div(o, RING), RING) * RING + lax.rem(z + lax.rem(o, RING), RING)

    def fro(o):
        return (
            lax.rem(y + RING - lax.div(o, RING), RING) * RING
            + lax.rem(z + RING - lax.rem(o, RING), RING)
        )

    def chip(c):
        return {"dom": c * 2 + k}

    partner = {"dom": r * 2 + (1 - k)}

    def seg(j):
        return {"segment": lax.rem(x + j, LAYERS)}

    def rcopy(src, dst, ssem, rsem, dev):
        return pltpu.make_async_remote_copy(
            src_ref=src, dst_ref=dst, send_sem=ssem, recv_sem=rsem, device_id=dev, device_id_type=MESH
        )

    def each(lo, hi, f):
        def body(i, c):
            f(i)
            return c
        lax.fori_loop(lo, hi, body, 0)

    load_f = pltpu.make_async_copy(feat_hbm.at[x], feat, loc_sem.at[0])
    load_t = pltpu.make_async_copy(tv_hbm.at[x], tv.at[r], loc_sem.at[1])
    load_f.start()
    load_t.start()

    barrier = pltpu.get_barrier_semaphore()
    each(1, CHIPS, lambda o: pl.semaphore_signal(barrier, inc=1, device_id=chip(to(o)), device_id_type=MESH))
    pl.semaphore_signal(barrier, inc=1, device_id=partner, device_id_type=MESH)
    for j in range(1, LAYERS):
        pl.semaphore_signal(barrier, inc=1, device_id=seg(j), device_id_type=MESH)

    load_f.wait()
    for b in range(D // TILE):
        xt[0, b * TILE:(b + 1) * TILE, :] = feat[:, b * TILE:(b + 1) * TILE].astype(F32).T.astype(BF16)
    load_t.wait()
    pl.semaphore_wait(barrier, CHIPS - 1 + 1 + LAYERS - 1)

    counter = [0]

    def at(h, da, db, lo, n):
        yy, zz = (y + db, z + da) if h == 0 else (y + da, z + db)
        c = lax.rem(yy + 2 * RING, RING) * RING + lax.rem(zz + 2 * RING, RING)
        return tv.at[c, pl.ds(2 * h + lo, n)]

    def ring_send(h, first, da, db, s, lo, n):
        along_z = (h == 0) == first
        if along_z:
            dev = chip(y * RING + lax.rem(z + s + RING, RING))
        else:
            dev = chip(lax.rem(y + s + RING, RING) * RING + z)
        i = counter[0]
        counter[0] += 1
        ref = at(h, da, db, lo, n)
        c = rcopy(ref, ref, tv_s.at[i], tv_r.at[i], dev)
        c.start()
        return c, (h, da, db, lo, n, i)

    def ring_wait(entry, first, s):
        h, da, db, lo, n, i = entry[1]
        da, db = (da - s, db) if first else (da, db - s)
        ref = at(h, da, db, lo, n)
        rcopy(ref, ref, tv_s.at[i], tv_r.at[i], partner).wait_recv()

    s1, s1b, s2, s2b = {}, {}, {}, {}

    def second(h, da):
        for s in (1, -1):
            s2[h, da, s] = ring_send(h, False, da, 0, s, 0, 2)

    def second_fwd(h, da):
        for s in (1, -1):
            ring_wait(s2[h, da, s], False, s)
            s2b[h, da, s] = ring_send(h, False, da, -s, s, 0 if s == 1 else 1, 1)

    for h in range(2):
        for s in (1, -1):
            s1[h, s] = ring_send(h, True, 0, 0, s, 0, 2)

    def t1_copy(l, o, c):
        return rcopy(
            xt.at[l, pl.ds(pl.multiple_of(c * FS, FS), FS)], xc.at[l, k, r], t1_s.at[l, o], t1_r.at[l, o], chip(c)
        )

    def t1_in(l, o):
        c = fro(o)
        return rcopy(xc.at[l, k, c], xc.at[l, k, c], t1_s.at[l, o], t1_r.at[l, o], partner)

    def fw_copy(l, o, kk):
        c = fro(o)
        return rcopy(xc.at[l, kk, c], xc.at[l, kk, c], fw_s.at[l, o], fw_r.at[l, o], partner)

    def t1_start(l):
        each(1, CHIPS, lambda o: t1_copy(l, o, to(o)).start())
        xc[l, k, r] = xt[l, pl.ds(pl.multiple_of(r * FS, FS), FS), :]
        fw_copy(l, 0, k).start()

    def t1_finish(l):
        def arrive(o):
            t1_in(l, o).wait_recv()
            fw_copy(l, o, k).start()
            xf[k * CHIPS + fro(o)] = xc[l, k, fro(o)].astype(F32)

        xf[k * CHIPS + r] = xc[l, k, r].astype(F32)
        each(1, CHIPS, arrive)

        def other(o):
            fw_copy(l, o, 1 - k).wait_recv()
            xf[(1 - k) * CHIPS + fro(o)] = xc[l, 1 - k, fro(o)].astype(F32)

        each(0, CHIPS, other)

    t1_start(0)
    for h in range(2):
        second(h, 0)

    lane = lax.broadcasted_iota(I32, (1, TILE), 1)
    for p in range(2 * CHIPS):
        live = lane < len_ref[x, 0, p]
        m1a[p % 2, p // 2:p // 2 + 1, :] = jnp.where(live, rows_ref[x, 0, p:p + 1, :], -1)
    pm = rcopy(m1a.at[1 - k], px, pm_s, pm_r, partner)
    pm.start()

    for b in range(D // TILE):
        cols = slice(b * TILE, (b + 1) * TILE)
        wp[x, cols, 0:D] = ws_ref[0, :, cols].astype(F32).T.astype(BF16)
        wp[x, cols, D:2 * D] = wn_ref[0, :, cols].astype(F32).T.astype(BF16)
        wp[x, cols, 2 * D:2 * D + AUX] = jnp.broadcast_to(gain_ref[:, cols].astype(F32), (AUX, TILE)).T.astype(BF16)
        wp[x, cols, 2 * D + AUX:2 * D + 2 * AUX] = (
            jnp.broadcast_to(bias_ref[:, cols].astype(F32), (AUX, TILE)).T.astype(BF16)
        )

    def w_copy(j):
        return rcopy(wp.at[x], wp.at[x], w_s.at[j], w_r.at[j], seg(j))

    for j in range(1, LAYERS):
        w_copy(j).start()

    pm.wait()
    m1b[...] = jnp.zeros(m1b.shape, I32)
    for c in range(CHIPS):
        m1b[c, pl.ds(k, 1), :] = m1a[k, c:c + 1, :]
        m1b[c, pl.ds(1 - k, 1), :] = px[c:c + 1, :]
    m1c[r] = m1b[r]

    def m1_copy(o):
        c = to(o)
        return rcopy(m1b.at[c], m1c.at[r], m_s.at[o], m_r.at[o], chip(c))

    each(1, CHIPS, lambda o: m1_copy(o).start())

    for h in range(2):
        for s in (1, -1):
            ring_wait(s1[h, s], True, s)
            s1b[h, s] = ring_send(h, True, -s, 0, s, 0 if s == 1 else 1, 1)
    for h in range(2):
        for s in (1, -1):
            second(h, -s)

    def m1_wait(o):
        rcopy(m1b.at[fro(o)], m1c.at[fro(o)], m_s.at[o], m_r.at[o], partner).wait_recv()
    each(1, CHIPS, m1_wait)

    picks = jnp.zeros((1, TILE), I32)
    for t in range(16):
        s = src_ref[x, t // 4, t % 4]
        q = jnp.maximum(s - 4, 0)
        row = m1c[q >> 1, pl.ds(q & 1, 1), :]
        row = jnp.where(s < 4, s * TILE + lane, row)
        row = jnp.where(t % 4 < cnt_ref[x, t // 4], row, -1)
        meta[r, t:t + 1, :] = row
        picks = jnp.where(lane == t, jnp.where(s < 4, k * CHIPS + r, (q & 1) * CHIPS + (q >> 1)), picks)
    meta[r, 16:24, :] = jnp.broadcast_to(picks, (8, TILE))

    def meta_copy(o, c, dev):
        return rcopy(meta.at[c], meta.at[c], mb_s.at[o], mb_r.at[o], dev)

    each(1, CHIPS, lambda o: meta_copy(o, r, chip(to(o))).start())

    for h in range(2):
        second_fwd(h, 0)
    for h in range(2):
        for s in (1, -1):
            ring_wait(s1b[h, s], True, s)
        second(h, 2)

    t1_finish(0)
    each(1, CHIPS, lambda o: meta_copy(o, fro(o), partner).wait_recv())
    move = pltpu.make_async_copy(meta.at[:, 16:24, :], qs, loc_sem.at[2])
    move.start()
    move.wait()

    for da in (1, -1, 2):
        for h in range(2):
            second_fwd(h, da)
    for (h, da, s), e in s2b.items():
        ring_wait(e, False, s)

    def gathered(q, idx):
        low = jnp.broadcast_to(idx & (TILE - 1), (FS, TILE))
        high = idx >> 7
        g = jnp.zeros((FS, TILE), F32)
        for b in range(ROWS // TILE):
            part = jnp.take_along_axis(xf[q, :, b * TILE:(b + 1) * TILE], low, axis=1)
            g = jnp.where(high == b, part, g)
        return g.astype(BF16)

    def t2_copy(l, o):
        c = to(o)
        return rcopy(aggs.at[l, c], agg.at[l, r], t2_s.at[l, o], t2_r.at[l, o], chip(c))

    def aggregate(l, o):
        c = to(o)
        for i in range(4):
            gs = [gathered(qs[c, 0, 4 * i + kk], meta[c, 4 * i + kk:4 * i + kk + 1, :]) for kk in range(4)]
            ts = [tv[c, i, kk] for kk in range(4)]
            a = lax.dot_general(
                jnp.concatenate(gs, axis=1), jnp.concatenate(ts, axis=1), (((1,), (1,)), ((), ())),
                preferred_element_type=F32,
            )
            aggs[l, c, :, i * TILE:(i + 1) * TILE] = a.astype(BF16)

    def out_local(l):
        return pltpu.make_async_copy(outr.at[l], out_hbm.at[0, x], loc_sem.at[3])

    def out_remote(l):
        j = lax.rem(x + LAYERS - l, LAYERS)
        return rcopy(outr.at[l], out_hbm.at[0, x], o_s.at[l], o_r.at[j], {"segment": l})

    def send_out(l):
        for b in range(D // TILE):
            outr[l, :, b * TILE:(b + 1) * TILE] = xt[l + 1, b * TILE:(b + 1) * TILE, :].astype(F32).T.astype(BF16)

        @pl.when(x == l)
        def _():
            out_local(l).start()

        @pl.when(x != l)
        def _():
            out_remote(l).start()

    half = ROWS // 2

    def layer(l):
        @pl.when(l > 0)
        def _():
            t1_start(l)
            send_out(l - 1)

        @pl.when(x != l)
        def _():
            j = lax.rem(x + LAYERS - l, LAYERS)
            rcopy(wp.at[l], wp.at[l], w_s.at[j], w_r.at[j], partner).wait_recv()

        for b in range(2):
            pre[b] = jnp.dot(
                wp[l, :, 0:D], xt[l, :, b * half:(b + 1) * half], preferred_element_type=F32
            )

        @pl.when(l > 0)
        def _():
            t1_finish(l)

        def one(o):
            aggregate(l, o)
            t2_copy(l, o).start()

        each(1, CHIPS, one)
        aggregate(l, 0)
        agg[l, r] = aggs[l, r]

        def got(o):
            c = fro(o)
            rcopy(aggs.at[l, c], agg.at[l, c], t2_s.at[l, o], t2_r.at[l, o], partner).wait_recv()
        each(1, CHIPS, got)
        for b in range(2):
            rhs = agg[l, :, :, b * half:(b + 1) * half].reshape(D, half)
            v = pre[b] + jnp.dot(wp[l, :, D:2 * D], rhs, preferred_element_type=F32)
            pre[b] = v - jnp.mean(v, axis=0, keepdims=True)
            v = pre[b]
            scale = lax.rsqrt(jnp.mean(v * v, axis=0, keepdims=True) + norm_eps)
            for e in range(2):
                cols = slice(e * AUX, (e + 1) * AUX)
                g = wp[l, :, 2 * D:2 * D + AUX].astype(F32)
                h = wp[l, :, 2 * D + AUX:2 * D + 2 * AUX].astype(F32)
                w = pre[b, :, cols] * scale[:, cols] * g + h
                xt[l + 1, :, b * half + e * AUX:b * half + (e + 1) * AUX] = jnp.maximum(w, 0.0).astype(BF16)

    each(0, LAYERS, layer)
    send_out(LAYERS - 1)

    for dct in (s1, s1b, s2, s2b):
        for c, _ in dct.values():
            c.wait_send()
    each(1, CHIPS, lambda o: m1_copy(o).wait_send())
    each(1, CHIPS, lambda o: meta_copy(o, r, chip(to(o))).wait_send())
    for j in range(1, LAYERS):
        w_copy(j).wait_send()

    def sent(l):
        def one(o):
            t1_copy(l, o, to(o)).wait_send()
            t2_copy(l, o).wait_send()
            fw_copy(l, o, k).wait_send()
        each(1, CHIPS, one)
        fw_copy(l, 0, k).wait_send()

        @pl.when(x == l)
        def _():
            out_local(l).wait()

        @pl.when(x != l)
        def _():
            out_remote(l).wait_send()

    each(0, LAYERS, sent)
    for j in range(1, LAYERS):
        c = lax.rem(x + j, LAYERS)
        rcopy(outr.at[0], out_hbm.at[0, c], o_s.at[0], o_r.at[j], partner).wait_recv()


def per_device(features, send_rows, send_len, tile_src, tile_count, tile_val, w_self, w_neigh, gain, bias):
    any_, vmem, smem = (pl.BlockSpec(memory_space=s) for s in (pl.ANY, pltpu.VMEM, pltpu.SMEM))
    dma = pltpu.SemaphoreType.DMA
    return pl.pallas_call(
        kernel,
        out_shape=jax.ShapeDtypeStruct((1, 4, ROWS, D), BF16),
        in_specs=[any_, vmem, smem, smem, smem, any_, vmem, vmem, vmem, vmem],
        out_specs=any_,
        scratch_shapes=[
            pltpu.VMEM((ROWS, D), BF16),
            pltpu.VMEM((LAYERS + 1, D, ROWS), BF16),
            pltpu.VMEM((LAYERS, D, 2 * D + 2 * AUX), BF16),
            pltpu.VMEM((CHIPS, 4, 4, TILE, TILE), BF16),
            pltpu.VMEM((CHIPS, 24, TILE), I32),
            pltpu.VMEM((2, CHIPS, TILE), I32),
            pltpu.VMEM((CHIPS, TILE), I32),
            pltpu.VMEM((CHIPS, 8, TILE), I32),
            pltpu.VMEM((CHIPS, 8, TILE), I32),
            pltpu.VMEM((LAYERS, 2, CHIPS, FS, ROWS), BF16),
            pltpu.VMEM((2 * CHIPS, FS, ROWS), F32),
            pltpu.VMEM((LAYERS, CHIPS, FS, ROWS), BF16),
            pltpu.VMEM((LAYERS, CHIPS, FS, ROWS), BF16),
            pltpu.VMEM((LAYERS, ROWS, D), BF16),
            pltpu.VMEM((2, D, ROWS // 2), F32),
            pltpu.SMEM((CHIPS, 8, TILE), I32),
            dma((4,)),
            dma((48,)), dma((48,)),
            dma((LAYERS, CHIPS)), dma((LAYERS, CHIPS)),
            dma((LAYERS, CHIPS)), dma((LAYERS, CHIPS)),
            dma((LAYERS, CHIPS)), dma((LAYERS, CHIPS)),
            dma((LAYERS,)), dma((LAYERS,)),
            dma((LAYERS,)), dma((LAYERS,)),
            dma((CHIPS,)), dma((CHIPS,)),
            dma((CHIPS,)), dma((CHIPS,)),
            dma, dma,
        ],
        compiler_params=pltpu.CompilerParams(collective_id=0, has_side_effects=True, vmem_limit_bytes=60 << 20),
    )(features, send_rows, send_len, tile_src, tile_count, tile_val, w_self, w_neigh, gain, bias)


def solution(mesh):
    in_specs = (
        P(None, "dom", None),
        P(None, "dom", None, None),
        P(None, "dom", None),
        P(None, "dom", None),
        P(None, "dom"),
        P(None, "dom", None, None, None),
        P("segment", None, None),
        P("segment", None, None),
        P("segment", None),
        P("segment", None),
    )
    out_specs = P("segment", None, "dom", None)
    return jax.shard_map(
        per_device, mesh=mesh, in_specs=in_specs, out_specs=out_specs, check_vma=False
    )
```

time: 850 us -> 176 us (0.21)
  waiting for transfers between devices: 429 us -> 0 us
  local copies, waits for them, and re-layouts: 231 us -> 3.05 us
  Pallas kernels: 0 us -> 173 us
  other arithmetic: 85.7 us -> 0 us
  starting transfers between devices: 56.6 us -> 0 us
  matrix products: 41 us -> 0 us
    all_to_all x7 -> x0, waiting for transfers between devices: 346 us -> none  [sage_layer(): lax.all_to_all(outgoing, 'dom', split_axis=0, concat_axis=0, tiled=True)]
    gather x35 -> x0, local copies, waits for them, and re-layouts: 203 us -> none  [the longest x7 122 us: sage_layer(): jnp.take(inputs, send_list.reshape(-1), axis=0)]
    pallas_call x0 -> x1, Pallas kernels: none -> 173 us  [per_device(): pl.pallas_call(kernel, out_shape=jax.ShapeDtypeStruct((1, 4, ROWS, D), BF...]
    ppermute x6 -> x0, waiting for transfers between devices: 83.1 us -> none  [passed_along(): return lax.ppermute(shard, axis, pairs)]
    all_to_all x7 -> x0, starting transfers between devices: 48.7 us -> none  [sage_layer(): lax.all_to_all(outgoing, 'dom', split_axis=0, concat_axis=0, tiled=True)]
    dot_general x42 -> x0, matrix products: 41 us -> none  [the longest x28 34.1 us: block_sum(): jnp.einsum('kij,kjd->id', masked, chosen, preferred_element_type=jnp.floa...]
    select_n x20 -> x0, other arithmetic: 35.7 us -> none  [the longest x7 18.1 us: sage_layer(): jnp.take(inputs, send_list.reshape(-1), axis=0)]
    concatenate x7 -> x0, other arithmetic: 33.2 us -> none  [sage_layer(): jnp.concatenate([inputs.reshape(block_count, tile_rows, feat_width), inco...]
  transfers between devices with their start and end apart: 13 -> 0, of which waited for: 13 -> 0; matrix products, arithmetic and copies ran while one was open for 3% -> 0% of each run, Pallas kernels for 0% -> 0%
where the time goes in v1:
time: 176 us
  Pallas kernels  173 us (98%)
  local copies, waits for them, and re-layouts  3.05 us (2%)
    pallas_call x1, Pallas kernels, per_device(): pl.pallas_call(kernel, out_shape=jax.ShapeDtypeStruct((1, 4, ROWS, D), BF...  173 us

profile of v1, /device:TPU:6, one launch (start us, length us, event | category | flops | bytes accessed | tf_op | source)
XLA Modules:
  0.0 175.8 jit_solution(8181434328491314823)
XLA Ops:
  0.0 172.7 %shard_map.100 = bf16[1,4,512,512]{3,2,1,0:T(8,128)(2,1)} custom-call(bf16[4,512,512]{2,1,0:T(8,128)(2,1)} %feat_hbm.1, s32[4,1,32,128]{3,2,1,0:T(8,128)} %rows_ref.1, s32[4,1,32]{2,1,0:T(1,128)} %len_ref.1, s32[4,4,4]{2,1,0:T(4,128)} %src_ref.1, s32[4,4]{1,0:T(4,128)} %cnt_ref.1, bf16[4,4,4,128,128]{4,3,2,1,0:T(8,128)(2,1)} %tv_hbm.1, ...), custom_call_target="tpu_custom_call" | custom-call | tf_op jit(solution)/shard_map/pallas_call | solution.py:364
  172.8 3.0 %copy.12 = bf16[1,4,512,512]{3,2,1,0:T(8,128)(2,1)} copy(bf16[1,4,512,512]{3,2,1,0:T(8,128)(2,1)} %shard_map.100) | data formatting | bytes 4194304

commit v2 on v1

--- a/solution.py
+++ b/solution.py
@@ -16,13 +16,16 @@
 D = 512
 FS = 32
 AUX = 128
+NH = 2
+HR = ROWS // NH
+BL = 4 // NH
 
 
 def kernel(
     feat_hbm, rows_ref, len_ref, src_ref, cnt_ref, tv_hbm, ws_ref, wn_ref, gain_ref, bias_ref,
     out_hbm,
     feat, xt, wp, tv, meta, m1a, px, m1b, m1c, xc, xf, aggs, agg, outr, pre, qs,
-    loc_sem, tv_s, tv_r, t1_s, t1_r, fw_s, fw_r, t2_s, t2_r, w_s, w_r, o_s, o_r, m_s, m_r, mb_s, mb_r, pm_s, pm_r,
+    loc_sem, ol_sem, tv_s, tv_r, t1_s, t1_r, fw_s, fw_r, t2_s, t2_r, w_s, w_r, wf_s, wf_r, o_s, o_r, m_s, m_r, mb_s, mb_r, pm_s, pm_r,
 ):
     x = lax.axis_index("segment")
     d = lax.axis_index("dom")
@@ -71,7 +74,9 @@
 
     load_f.wait()
     for b in range(D // TILE):
-        xt[0, b * TILE:(b + 1) * TILE, :] = feat[:, b * TILE:(b + 1) * TILE].astype(F32).T.astype(BF16)
+        for h in range(NH):
+            part = feat[h * HR:(h + 1) * HR, b * TILE:(b + 1) * TILE]
+            xt[0, h, b * TILE:(b + 1) * TILE, :] = part.astype(F32).T.astype(BF16)
     load_t.wait()
     pl.semaphore_wait(barrier, CHIPS - 1 + 1 + LAYERS - 1)
 
@@ -116,40 +121,51 @@
         for s in (1, -1):
             s1[h, s] = ring_send(h, True, 0, 0, s, 0, 2)
 
-    def t1_copy(l, o, c):
+    def t1_copy(l, h, o, c):
         return rcopy(
-            xt.at[l, pl.ds(pl.multiple_of(c * FS, FS), FS)], xc.at[l, k, r], t1_s.at[l, o], t1_r.at[l, o], chip(c)
+            xt.at[l, h, pl.ds(pl.multiple_of(c * FS, FS), FS)], xc.at[l, h, k, r],
+            t1_s.at[l, h, o], t1_r.at[l, h, o], chip(c),
         )
 
-    def t1_in(l, o):
-        c = fro(o)
-        return rcopy(xc.at[l, k, c], xc.at[l, k, c], t1_s.at[l, o], t1_r.at[l, o], partner)
-
-    def fw_copy(l, o, kk):
-        c = fro(o)
-        return rcopy(xc.at[l, kk, c], xc.at[l, kk, c], fw_s.at[l, o], fw_r.at[l, o], partner)
-
-    def t1_start(l):
-        each(1, CHIPS, lambda o: t1_copy(l, o, to(o)).start())
-        xc[l, k, r] = xt[l, pl.ds(pl.multiple_of(r * FS, FS), FS), :]
-        fw_copy(l, 0, k).start()
+    def t1_in(l, h, o):
+        ref = xc.at[l, h, k, fro(o)]
+        return rcopy(ref, ref, t1_s.at[l, h, o], t1_r.at[l, h, o], partner)
+
+    def row_of(dy):
+        return lax.rem(y + RING - dy, RING)
+
+    def fw_copy(l, h, dy, kk):
+        ref = xc.at[l, h, kk, pl.ds(row_of(dy) * RING, RING)]
+        return rcopy(ref, ref, fw_s.at[l, h, dy], fw_r.at[l, h, dy], partner)
+
+    def t1_start(l, h):
+        each(1, CHIPS, lambda o: t1_copy(l, h, o, to(o)).start())
+        xc[l, h, k, r] = xt[l, h, pl.ds(pl.multiple_of(r * FS, FS), FS), :]
+
+    def widen(l, h, dy, kk):
+        def one(e):
+            c = row_of(dy) * RING + e
+            xf[kk * CHIPS + c, :, h * HR:(h + 1) * HR] = xc[l, h, kk, c].astype(F32)
+        each(0, RING, one)
 
     def t1_finish(l):
-        def arrive(o):
-            t1_in(l, o).wait_recv()
-            fw_copy(l, o, k).start()
-            xf[k * CHIPS + fro(o)] = xc[l, k, fro(o)].astype(F32)
-
-        xf[k * CHIPS + r] = xc[l, k, r].astype(F32)
-        each(1, CHIPS, arrive)
-
-        def other(o):
-            fw_copy(l, o, 1 - k).wait_recv()
-            xf[(1 - k) * CHIPS + fro(o)] = xc[l, 1 - k, fro(o)].astype(F32)
-
-        each(0, CHIPS, other)
-
-    t1_start(0)
+        for h in range(NH):
+            def arrive(dy):
+                @pl.when(dy > 0)
+                def _():
+                    t1_in(l, h, dy * RING).wait_recv()
+                each(1, RING, lambda dz: t1_in(l, h, dy * RING + dz).wait_recv())
+                fw_copy(l, h, dy, k).start()
+                widen(l, h, dy, k)
+            each(0, RING, arrive)
+        for h in range(NH):
+            def other(dy):
+                fw_copy(l, h, dy, 1 - k).wait_recv()
+                widen(l, h, dy, 1 - k)
+            each(0, RING, other)
+
+    for h in range(NH):
+        t1_start(0, h)
     for h in range(2):
         second(h, 0)
 
@@ -169,8 +185,23 @@
             jnp.broadcast_to(bias_ref[:, cols].astype(F32), (AUX, TILE)).T.astype(BF16)
         )
 
+    def w_part(l, kk):
+        return wp.at[l, pl.ds(pl.multiple_of(kk * (D // 2), D // 2), D // 2)]
+
     def w_copy(j):
-        return rcopy(wp.at[x], wp.at[x], w_s.at[j], w_r.at[j], seg(j))
+        return rcopy(w_part(x, k), w_part(x, k), w_s.at[j], w_r.at[j], seg(j))
+
+    def w_from(j):
+        return lax.rem(x + LAYERS - j, LAYERS)
+
+    def wf_copy(j, kk):
+        ref = w_part(w_from(j), kk)
+        return rcopy(ref, ref, wf_s.at[j], wf_r.at[j], partner)
+
+    def w_forward(j):
+        ref = w_part(w_from(j), k)
+        rcopy(ref, ref, w_s.at[j], w_r.at[j], partner).wait_recv()
+        wf_copy(j, k).start()
 
     for j in range(1, LAYERS):
         w_copy(j).start()
@@ -187,6 +218,83 @@
         return rcopy(m1b.at[c], m1c.at[r], m_s.at[o], m_r.at[o], chip(c))
 
     each(1, CHIPS, lambda o: m1_copy(o).start())
+
+    def gathered(q, idx):
+        low = jnp.broadcast_to(idx & (TILE - 1), (FS, TILE))
+        high = idx >> 7
+        g = jnp.zeros((FS, TILE), F32)
+        for b in range(ROWS // TILE):
+            part = jnp.take_along_axis(xf[q, :, b * TILE:(b + 1) * TILE], low, axis=1)
+            g = jnp.where(high == b, part, g)
+        return g.astype(BF16)
+
+    def t2_copy(l, h, o):
+        c = to(o)
+        return rcopy(aggs.at[l, h, c], agg.at[l, h, r], t2_s.at[l, h, o], t2_r.at[l, h, o], chip(c))
+
+    def send_back(l, h, o):
+        own = isinstance(o, int) and o == 0
+        c = to(o)
+        for b in range(BL):
+            i = h * BL + b
+            gs = [gathered(qs[c, 0, 4 * i + kk], meta[c, 4 * i + kk:4 * i + kk + 1, :]) for kk in range(4)]
+            ts = [tv[c, i, kk] for kk in range(4)]
+            a = lax.dot_general(
+                jnp.concatenate(gs, axis=1), jnp.concatenate(ts, axis=1), (((1,), (1,)), ((), ())),
+                preferred_element_type=F32,
+            )
+            dst = agg if own else aggs
+            dst[l, h, c, :, b * TILE:(b + 1) * TILE] = a.astype(BF16)
+        if not own:
+            t2_copy(l, h, o).start()
+
+    def out_rows(l, h):
+        return outr.at[l, pl.ds(h * HR, HR)], out_hbm.at[0, x, pl.ds(h * HR, HR)]
+
+    def out_local(l, h):
+        src, dst = out_rows(l, h)
+        return pltpu.make_async_copy(src, dst, ol_sem.at[h])
+
+    def out_remote(l, h):
+        j = lax.rem(x + LAYERS - l, LAYERS)
+        src, dst = out_rows(l, h)
+        return rcopy(src, dst, o_s.at[l, h], o_r.at[j, h], {"segment": l})
+
+    def send_out(l, h):
+        for b in range(D // TILE):
+            part = xt[l + 1, h, b * TILE:(b + 1) * TILE, :]
+            outr[l, h * HR:(h + 1) * HR, b * TILE:(b + 1) * TILE] = part.astype(F32).T.astype(BF16)
+
+        @pl.when(x == l)
+        def _():
+            out_local(l, h).start()
+
+        @pl.when(x != l)
+        def _():
+            out_remote(l, h).start()
+
+    def dense(l, h):
+        def got(o):
+            ref = agg.at[l, h, fro(o)]
+            rcopy(ref, ref, t2_s.at[l, h, o], t2_r.at[l, h, o], partner).wait_recv()
+        each(1, CHIPS, got)
+        rhs = agg[l, h].reshape(D, HR)
+        v = pre[h] + jnp.dot(wp[l, :, D:2 * D], rhs, preferred_element_type=F32)
+        pre[h] = v - jnp.mean(v, axis=0, keepdims=True)
+        v = pre[h]
+        scale = lax.rsqrt(jnp.mean(v * v, axis=0, keepdims=True) + norm_eps)
+        g = wp[l, :, 2 * D:2 * D + AUX].astype(F32)
+        b = wp[l, :, 2 * D + AUX:2 * D + 2 * AUX].astype(F32)
+        for e in range(HR // AUX):
+            cols = slice(e * AUX, (e + 1) * AUX)
+            w = pre[h, :, cols] * scale[:, cols] * g + b
+            xt[l + 1, h, :, cols] = jnp.maximum(w, 0.0).astype(BF16)
+
+    def advance(l, h):
+        @pl.when(l < LAYERS - 1)
+        def _():
+            t1_start(l + 1, h)
+        send_out(l, h)
 
     for h in range(2):
         for s in (1, -1):
@@ -229,104 +337,59 @@
     move.start()
     move.wait()
 
-    for da in (1, -1, 2):
+    def arrived(names):
+        for name in names:
+            ring_wait(s2b[name], False, name[2])
+
+    def first_layer(offsets):
+        for dy, dz in offsets:
+            o = dy % RING * RING + dz % RING
+            for h in range(NH):
+                send_back(0, h, o)
+
+    first_layer([(0, 0), (0, 1), (0, -1), (1, 0), (-1, 0)])
+    for da in (1, -1):
         for h in range(2):
             second_fwd(h, da)
-    for (h, da, s), e in s2b.items():
-        ring_wait(e, False, s)
-
-    def gathered(q, idx):
-        low = jnp.broadcast_to(idx & (TILE - 1), (FS, TILE))
-        high = idx >> 7
-        g = jnp.zeros((FS, TILE), F32)
-        for b in range(ROWS // TILE):
-            part = jnp.take_along_axis(xf[q, :, b * TILE:(b + 1) * TILE], low, axis=1)
-            g = jnp.where(high == b, part, g)
-        return g.astype(BF16)
-
-    def t2_copy(l, o):
-        c = to(o)
-        return rcopy(aggs.at[l, c], agg.at[l, r], t2_s.at[l, o], t2_r.at[l, o], chip(c))
-
-    def aggregate(l, o):
-        c = to(o)
-        for i in range(4):
-            gs = [gathered(qs[c, 0, 4 * i + kk], meta[c, 4 * i + kk:4 * i + kk + 1, :]) for kk in range(4)]
-            ts = [tv[c, i, kk] for kk in range(4)]
-            a = lax.dot_general(
-                jnp.concatenate(gs, axis=1), jnp.concatenate(ts, axis=1), (((1,), (1,)), ((), ())),
-                preferred_element_type=F32,
-            )
-            aggs[l, c, :, i * TILE:(i + 1) * TILE] = a.astype(BF16)
-
-    def out_local(l):
-        return pltpu.make_async_copy(outr.at[l], out_hbm.at[0, x], loc_sem.at[3])
-
-    def out_remote(l):
-        j = lax.rem(x + LAYERS - l, LAYERS)
-        return rcopy(outr.at[l], out_hbm.at[0, x], o_s.at[l], o_r.at[j], {"segment": l})
-
-    def send_out(l):
-        for b in range(D // TILE):
-            outr[l, :, b * TILE:(b + 1) * TILE] = xt[l + 1, b * TILE:(b + 1) * TILE, :].astype(F32).T.astype(BF16)
-
-        @pl.when(x == l)
-        def _():
-            out_local(l).start()
-
-        @pl.when(x != l)
-        def _():
-            out_remote(l).start()
-
-    half = ROWS // 2
-
-    def layer(l):
-        @pl.when(l > 0)
-        def _():
-            t1_start(l)
-            send_out(l - 1)
-
+    arrived([(h, 0, s) for h in range(2) for s in (1, -1)])
+    first_layer([(0, 2), (2, 0)])
+    first_layer([(1, 1), (-1, -1), (1, -1), (-1, 1)])
+    for h in range(2):
+        second_fwd(h, 2)
+    arrived([(h, da, s) for da in (1, -1) for h in range(2) for s in (1, -1)])
+    first_layer([(2, 1), (2, -1), (1, 2), (-1, 2)])
+    arrived([(h, 2, s) for h in range(2) for s in (1, -1)])
+    first_layer([(2, 2)])
+    for j in range(1, LAYERS):
+        w_forward(j)
+
+    def own_part(l):
         @pl.when(x != l)
         def _():
             j = lax.rem(x + LAYERS - l, LAYERS)
-            rcopy(wp.at[l], wp.at[l], w_s.at[j], w_r.at[j], partner).wait_recv()
-
-        for b in range(2):
-            pre[b] = jnp.dot(
-                wp[l, :, 0:D], xt[l, :, b * half:(b + 1) * half], preferred_element_type=F32
-            )
-
-        @pl.when(l > 0)
-        def _():
-            t1_finish(l)
-
-        def one(o):
-            aggregate(l, o)
-            t2_copy(l, o).start()
-
-        each(1, CHIPS, one)
-        aggregate(l, 0)
-        agg[l, r] = aggs[l, r]
-
-        def got(o):
-            c = fro(o)
-            rcopy(aggs.at[l, c], agg.at[l, c], t2_s.at[l, o], t2_r.at[l, o], partner).wait_recv()
-        each(1, CHIPS, got)
-        for b in range(2):
-            rhs = agg[l, :, :, b * half:(b + 1) * half].reshape(D, half)
-            v = pre[b] + jnp.dot(wp[l, :, D:2 * D], rhs, preferred_element_type=F32)
-            pre[b] = v - jnp.mean(v, axis=0, keepdims=True)
-            v = pre[b]
-            scale = lax.rsqrt(jnp.mean(v * v, axis=0, keepdims=True) + norm_eps)
-            for e in range(2):
-                cols = slice(e * AUX, (e + 1) * AUX)
-                g = wp[l, :, 2 * D:2 * D + AUX].astype(F32)
-                h = wp[l, :, 2 * D + AUX:2 * D + 2 * AUX].astype(F32)
-                w = pre[b, :, cols] * scale[:, cols] * g + h
-                xt[l + 1, :, b * half + e * AUX:b * half + (e + 1) * AUX] = jnp.maximum(w, 0.0).astype(BF16)
-
-    each(0, LAYERS, layer)
-    send_out(LAYERS - 1)
+            wf_copy(j, 1 - k).wait_recv()
+
+        for h in range(NH):
+            pre[h] = jnp.dot(wp[l, :, 0:D], xt[l, h], preferred_element_type=F32)
+
+    own_part(0)
+    for h in range(NH):
+        dense(0, h)
+        advance(0, h)
+
+    def layer(l):
+        own_part(l)
+        t1_finish(l)
+        for h in range(NH):
+            each(1, CHIPS, lambda o: send_back(l, h, o))
+            send_back(l, h, 0)
+            if h > 0:
+                dense(l, h - 1)
+                advance(l, h - 1)
+        dense(l, NH - 1)
+        advance(l, NH - 1)
+
+    each(1, LAYERS, layer)
 
     for dct in (s1, s1b, s2, s2b):
         for c, _ in dct.values():
@@ -335,27 +398,30 @@
     each(1, CHIPS, lambda o: meta_copy(o, r, chip(to(o))).wait_send())
     for j in range(1, LAYERS):
         w_copy(j).wait_send()
+        wf_copy(j, k).wait_send()
 
     def sent(l):
-        def one(o):
-            t1_copy(l, o, to(o)).wait_send()
-            t2_copy(l, o).wait_send()
-            fw_copy(l, o, k).wait_send()
-        each(1, CHIPS, one)
-        fw_copy(l, 0, k).wait_send()
-
-        @pl.when(x == l)
-        def _():
-            out_local(l).wait()
-
-        @pl.when(x != l)
-        def _():
-            out_remote(l).wait_send()
+        for h in range(NH):
+            def one(o):
+                t1_copy(l, h, o, to(o)).wait_send()
+                t2_copy(l, h, o).wait_send()
+            each(1, CHIPS, one)
+            each(0, RING, lambda dy: fw_copy(l, h, dy, k).wait_send())
+
+            @pl.when(x == l)
+            def _():
+                out_local(l, h).wait()
+
+            @pl.when(x != l)
+            def _():
+                out_remote(l, h).wait_send()
 
     each(0, LAYERS, sent)
     for j in range(1, LAYERS):
         c = lax.rem(x + j, LAYERS)
-        rcopy(outr.at[0], out_hbm.at[0, c], o_s.at[0], o_r.at[j], partner).wait_recv()
+        for h in range(NH):
+            src, _ = out_rows(0, h)
+            rcopy(src, out_hbm.at[0, c, pl.ds(h * HR, HR)], o_s.at[0, h], o_r.at[j, h], partner).wait_recv()
 
 
 def per_device(features, send_rows, send_len, tile_src, tile_count, tile_val, w_self, w_neigh, gain, bias):
@@ -368,7 +434,7 @@
         out_specs=any_,
         scratch_shapes=[
             pltpu.VMEM((ROWS, D), BF16),
-            pltpu.VMEM((LAYERS + 1, D, ROWS), BF16),
+            pltpu.VMEM((LAYERS + 1, NH, D, HR), BF16),
             pltpu.VMEM((LAYERS, D, 2 * D + 2 * AUX), BF16),
             pltpu.VMEM((CHIPS, 4, 4, TILE, TILE), BF16),
             pltpu.VMEM((CHIPS, 24, TILE), I32),
@@ -376,20 +442,21 @@
             pltpu.VMEM((CHIPS, TILE), I32),
             pltpu.VMEM((CHIPS, 8, TILE), I32),
             pltpu.VMEM((CHIPS, 8, TILE), I32),
-            pltpu.VMEM((LAYERS, 2, CHIPS, FS, ROWS), BF16),
+            pltpu.VMEM((LAYERS, NH, 2, CHIPS, FS, HR), BF16),
             pltpu.VMEM((2 * CHIPS, FS, ROWS), F32),
-            pltpu.VMEM((LAYERS, CHIPS, FS, ROWS), BF16),
-            pltpu.VMEM((LAYERS, CHIPS, FS, ROWS), BF16),
+            pltpu.VMEM((LAYERS, NH, CHIPS, FS, HR), BF16),
+            pltpu.VMEM((LAYERS, NH, CHIPS, FS, HR), BF16),
             pltpu.VMEM((LAYERS, ROWS, D), BF16),
-            pltpu.VMEM((2, D, ROWS // 2), F32),
+            pltpu.VMEM((NH, D, HR), F32),
             pltpu.SMEM((CHIPS, 8, TILE), I32),
-            dma((4,)),
+            dma((3,)), dma((NH,)),
             dma((48,)), dma((48,)),
-            dma((LAYERS, CHIPS)), dma((LAYERS, CHIPS)),
-            dma((LAYERS, CHIPS)), dma((LAYERS, CHIPS)),
-            dma((LAYERS, CHIPS)), dma((LAYERS, CHIPS)),
+            dma((LAYERS, NH, CHIPS)), dma((LAYERS, NH, CHIPS)),
+            dma((LAYERS, NH, RING)), dma((LAYERS, NH, RING)),
+            dma((LAYERS, NH, CHIPS)), dma((LAYERS, NH, CHIPS)),
             dma((LAYERS,)), dma((LAYERS,)),
             dma((LAYERS,)), dma((LAYERS,)),
+            dma((LAYERS, NH)), dma((LAYERS, NH)),
             dma((CHIPS,)), dma((CHIPS,)),
             dma((CHIPS,)), dma((CHIPS,)),
             dma, dma,

time: 176 us -> 170 us (0.966)
  Pallas kernels: 173 us -> 167 us
    pallas_call x1, Pallas kernels: 173 us -> 167 us  [per_device(): pl.pallas_call(kernel, out_shape=jax.ShapeDtypeStruct((1, 4, ROWS, D), BF...]
where the time goes in v2:
time: 170 us
  Pallas kernels  167 us (98%)
  local copies, waits for them, and re-layouts  3.05 us (2%)
    pallas_call x1, Pallas kernels, per_device(): pl.pallas_call(kernel, out_shape=jax.ShapeDtypeStruct((1, 4, ROWS, D), BF...  167 us

profile of v2, /device:TPU:6, one launch (start us, length us, event | category | flops | bytes accessed | tf_op | source)
XLA Modules:
  0.0 169.9 jit_solution(7474823660941328151)
XLA Ops:
  0.0 166.9 %shard_map.100 = bf16[1,4,512,512]{3,2,1,0:T(8,128)(2,1)} custom-call(bf16[4,512,512]{2,1,0:T(8,128)(2,1)} %feat_hbm.1, s32[4,1,32,128]{3,2,1,0:T(8,128)} %rows_ref.1, s32[4,1,32]{2,1,0:T(1,128)} %len_ref.1, s32[4,4,4]{2,1,0:T(4,128)} %src_ref.1, s32[4,4]{1,0:T(4,128)} %cnt_ref.1, bf16[4,4,4,128,128]{4,3,2,1,0:T(8,128)(2,1)} %tv_hbm.1, ...), custom_call_target="tpu_custom_call" | custom-call | tf_op jit(solution)/shard_map/pallas_call | solution.py:430
  166.9 3.0 %copy.12 = bf16[1,4,512,512]{3,2,1,0:T(8,128)(2,1)} copy(bf16[1,4,512,512]{3,2,1,0:T(8,128)(2,1)} %shard_map.100) | data formatting | bytes 4194304

commit v3 on v2

--- a/solution.py
+++ b/solution.py
@@ -24,8 +24,8 @@
 def kernel(
     feat_hbm, rows_ref, len_ref, src_ref, cnt_ref, tv_hbm, ws_ref, wn_ref, gain_ref, bias_ref,
     out_hbm,
-    feat, xt, wp, tv, meta, m1a, px, m1b, m1c, xc, xf, aggs, agg, outr, pre, qs,
-    loc_sem, ol_sem, tv_s, tv_r, t1_s, t1_r, fw_s, fw_r, t2_s, t2_r, w_s, w_r, wf_s, wf_r, o_s, o_r, m_s, m_r, mb_s, mb_r, pm_s, pm_r,
+    feat, tvs, ga, gb, relay, xt, wp, tv, meta, m1a, px, m1b, m1c, xc, xf, aggs, agg, outr, pre, qs,
+    loc_sem, ol_sem, rl_s, rl_r, tv_s, tv_r, t1_s, t1_r, fw_s, fw_r, t2_s, t2_r, w_s, w_r, wf_s, wf_r, o_s, o_r, m_s, m_r, mb_s, mb_r, pm_s, pm_r,
 ):
     x = lax.axis_index("segment")
     d = lax.axis_index("dom")
@@ -62,7 +62,7 @@
         lax.fori_loop(lo, hi, body, 0)
 
     load_f = pltpu.make_async_copy(feat_hbm.at[x], feat, loc_sem.at[0])
-    load_t = pltpu.make_async_copy(tv_hbm.at[x], tv.at[r], loc_sem.at[1])
+    load_t = pltpu.make_async_copy(tv_hbm.at[x], tvs, loc_sem.at[1])
     load_f.start()
     load_t.start()
 
@@ -72,12 +72,13 @@
     for j in range(1, LAYERS):
         pl.semaphore_signal(barrier, inc=1, device_id=seg(j), device_id_type=MESH)
 
-    load_f.wait()
-    for b in range(D // TILE):
-        for h in range(NH):
-            part = feat[h * HR:(h + 1) * HR, b * TILE:(b + 1) * TILE]
-            xt[0, h, b * TILE:(b + 1) * TILE, :] = part.astype(F32).T.astype(BF16)
+    def transpose_tiles(h):
+        for i in range(2 * h, 2 * h + 2):
+            for kk in range(4):
+                tv[r, i, kk] = tvs[i, kk].astype(F32).T.astype(BF16)
+
     load_t.wait()
+    transpose_tiles(0)
     pl.semaphore_wait(barrier, CHIPS - 1 + 1 + LAYERS - 1)
 
     counter = [0]
@@ -118,8 +119,15 @@
             s2b[h, da, s] = ring_send(h, False, da, -s, s, 0 if s == 1 else 1, 1)
 
     for h in range(2):
+        if h == 1:
+            transpose_tiles(1)
         for s in (1, -1):
             s1[h, s] = ring_send(h, True, 0, 0, s, 0, 2)
+    load_f.wait()
+    for b in range(D // TILE):
+        for h in range(NH):
+            part = feat[h * HR:(h + 1) * HR, b * TILE:(b + 1) * TILE]
+            xt[0, h, b * TILE:(b + 1) * TILE, :] = part.astype(F32).T.astype(BF16)
 
     def t1_copy(l, h, o, c):
         return rcopy(
@@ -232,21 +240,40 @@
         c = to(o)
         return rcopy(aggs.at[l, h, c], agg.at[l, h, r], t2_s.at[l, h, o], t2_r.at[l, h, o], chip(c))
 
-    def send_back(l, h, o):
-        own = isinstance(o, int) and o == 0
+    def gather(o, blocks, buf):
         c = to(o)
-        for b in range(BL):
-            i = h * BL + b
-            gs = [gathered(qs[c, 0, 4 * i + kk], meta[c, 4 * i + kk:4 * i + kk + 1, :]) for kk in range(4)]
-            ts = [tv[c, i, kk] for kk in range(4)]
-            a = lax.dot_general(
-                jnp.concatenate(gs, axis=1), jnp.concatenate(ts, axis=1), (((1,), (1,)), ((), ())),
-                preferred_element_type=F32,
+        for b, i in enumerate(blocks):
+            for kk in range(4):
+                t = 4 * i + kk
+                buf[:, (4 * b + kk) * TILE:(4 * b + kk + 1) * TILE] = gathered(qs[c, 0, t], meta[c, t:t + 1, :])
+
+    def multiply(l, o, blocks, buf, dst):
+        c = to(o)
+        for b, i in enumerate(blocks):
+            a = jnp.dot(
+                buf[:, 4 * b * TILE:4 * (b + 1) * TILE], tv[c, i].reshape(4 * TILE, TILE), preferred_element_type=F32
             )
-            dst = agg if own else aggs
-            dst[l, h, c, :, b * TILE:(b + 1) * TILE] = a.astype(BF16)
-        if not own:
+            e = i % BL
+            dst[l, i // BL, c, :, e * TILE:(e + 1) * TILE] = a.astype(BF16)
+
+    def aggregate(l, h):
+        blocks = range(h * BL, (h + 1) * BL)
+        gather(1, blocks, ga)
+
+        def two(t):
+            o = 2 * t + 1
+            multiply(l, o, blocks, ga, aggs)
+            gather(o + 1, blocks, gb)
             t2_copy(l, h, o).start()
+            multiply(l, o + 1, blocks, gb, aggs)
+            gather(o + 2, blocks, ga)
+            t2_copy(l, h, o + 1).start()
+
+        each(0, CHIPS // 2 - 1, two)
+        multiply(l, CHIPS - 1, blocks, ga, aggs)
+        gather(0, blocks, gb)
+        t2_copy(l, h, CHIPS - 1).start()
+        multiply(l, 0, blocks, gb, agg)
 
     def out_rows(l, h):
         return outr.at[l, pl.ds(h * HR, HR)], out_hbm.at[0, x, pl.ds(h * HR, HR)]
@@ -260,6 +287,16 @@
         src, dst = out_rows(l, h)
         return rcopy(src, dst, o_s.at[l, h], o_r.at[j, h], {"segment": l})
 
+    last = LAYERS - 1
+
+    def relay_in(h):
+        return rcopy(
+            outr.at[last, pl.ds(h * HR, HR)], relay, rl_s.at[h], rl_r, {"segment": last - 1 if h == 0 else 0}
+        )
+
+    def relay_out(h):
+        return rcopy(relay, out_hbm.at[0, 1, pl.ds(h * HR, HR)], rl_s.at[NH], o_r.at[2, h], {"segment": last})
+
     def send_out(l, h):
         for b in range(D // TILE):
             part = xt[l + 1, h, b * TILE:(b + 1) * TILE, :]
@@ -269,9 +306,15 @@
         def _():
             out_local(l, h).start()
 
-        @pl.when(x != l)
+        far = (x == 1) & (l == last)
+
+        @pl.when((x != l) & jnp.logical_not(far))
         def _():
             out_remote(l, h).start()
+
+        @pl.when(far)
+        def _():
+            relay_in(h).start()
 
     def dense(l, h):
         def got(o):
@@ -341,25 +384,36 @@
         for name in names:
             ring_wait(s2b[name], False, name[2])
 
-    def first_layer(offsets):
-        for dy, dz in offsets:
-            o = dy % RING * RING + dz % RING
-            for h in range(NH):
-                send_back(0, h, o)
-
-    first_layer([(0, 0), (0, 1), (0, -1), (1, 0), (-1, 0)])
+    order = [
+        (0, 0), (0, 1), (0, -1), (1, 0), (-1, 0), (0, 2), (2, 0), (1, 1), (-1, -1), (1, -1), (-1, 1),
+        (2, 1), (2, -1), (1, 2), (-1, 2), (2, 2),
+    ]
+    offsets = [dy % RING * RING + dz % RING for dy, dz in order]
+    bufs = (ga, gb)
+    gather(offsets[0], range(4), ga)
+
+    def first_layer(lo, hi):
+        for u in range(lo, hi):
+            o = offsets[u]
+            multiply(0, o, range(4), bufs[u % 2], aggs if o else agg)
+            if u + 1 < CHIPS:
+                gather(offsets[u + 1], range(4), bufs[(u + 1) % 2])
+            if o:
+                for h in range(NH):
+                    t2_copy(0, h, o).start()
+
+    first_layer(0, 5)
     for da in (1, -1):
         for h in range(2):
             second_fwd(h, da)
     arrived([(h, 0, s) for h in range(2) for s in (1, -1)])
-    first_layer([(0, 2), (2, 0)])
-    first_layer([(1, 1), (-1, -1), (1, -1), (-1, 1)])
+    first_layer(5, 11)
     for h in range(2):
         second_fwd(h, 2)
     arrived([(h, da, s) for da in (1, -1) for h in range(2) for s in (1, -1)])
-    first_layer([(2, 1), (2, -1), (1, 2), (-1, 2)])
+    first_layer(11, 15)
     arrived([(h, 2, s) for h in range(2) for s in (1, -1)])
-    first_layer([(2, 2)])
+    first_layer(15, 16)
     for j in range(1, LAYERS):
         w_forward(j)
 
@@ -381,8 +435,7 @@
         own_part(l)
         t1_finish(l)
         for h in range(NH):
-            each(1, CHIPS, lambda o: send_back(l, h, o))
-            send_back(l, h, 0)
+            aggregate(l, h)
             if h > 0:
                 dense(l, h - 1)
                 advance(l, h - 1)
@@ -390,6 +443,13 @@
         advance(l, NH - 1)
 
     each(1, LAYERS, layer)
+
+    for h, at_x in ((0, last - 1), (1, 0)):
+        @pl.when(x == at_x)
+        def _():
+            relay_in(h).wait_recv()
+            relay_out(h).start()
+            relay_out(h).wait_send()
 
     for dct in (s1, s1b, s2, s2b):
         for c, _ in dct.values():
@@ -412,9 +472,15 @@
             def _():
                 out_local(l, h).wait()
 
-            @pl.when(x != l)
+            far = (x == 1) & (l == last)
+
+            @pl.when((x != l) & jnp.logical_not(far))
             def _():
                 out_remote(l, h).wait_send()
+
+            @pl.when(far)
+            def _():
+                relay_in(h).wait_send()
 
     each(0, LAYERS, sent)
     for j in range(1, LAYERS):
@@ -434,6 +500,10 @@
         out_specs=any_,
         scratch_shapes=[
             pltpu.VMEM((ROWS, D), BF16),
+            pltpu.VMEM((4, 4, TILE, TILE), BF16),
+            pltpu.VMEM((FS, 16 * TILE), BF16),
+            pltpu.VMEM((FS, 16 * TILE), BF16),
+            pltpu.VMEM((HR, D), BF16),
             pltpu.VMEM((LAYERS + 1, NH, D, HR), BF16),
             pltpu.VMEM((LAYERS, D, 2 * D + 2 * AUX), BF16),
             pltpu.VMEM((CHIPS, 4, 4, TILE, TILE), BF16),
@@ -449,7 +519,7 @@
             pltpu.VMEM((LAYERS, ROWS, D), BF16),
             pltpu.VMEM((NH, D, HR), F32),
             pltpu.SMEM((CHIPS, 8, TILE), I32),
-            dma((3,)), dma((NH,)),
+            dma((3,)), dma((NH,)), dma((NH + 1,)), dma,
             dma((48,)), dma((48,)),
             dma((LAYERS, NH, CHIPS)), dma((LAYERS, NH, CHIPS)),
             dma((LAYERS, NH, RING)), dma((LAYERS, NH, RING)),

time: 170 us -> 154 us (0.906)
  Pallas kernels: 167 us -> 151 us
    pallas_call x1, Pallas kernels: 167 us -> 151 us  [per_device(): pl.pallas_call(kernel, out_shape=jax.ShapeDtypeStruct((1, 4, ROWS, D), BF...]
where the time goes in v3:
time: 154 us
  Pallas kernels  151 us (98%)
  local copies, waits for them, and re-layouts  3.05 us (2%)
    pallas_call x1, Pallas kernels, per_device(): pl.pallas_call(kernel, out_shape=jax.ShapeDtypeStruct((1, 4, ROWS, D), BF...  151 us

profile of v3, /device:TPU:6, one launch (start us, length us, event | category | flops | bytes accessed | tf_op | source)
XLA Modules:
  0.0 154.0 jit_solution(11546717667405914572)
XLA Ops:
  0.0 151.0 %shard_map.100 = bf16[1,4,512,512]{3,2,1,0:T(8,128)(2,1)} custom-call(bf16[4,512,512]{2,1,0:T(8,128)(2,1)} %feat_hbm.1, s32[4,1,32,128]{3,2,1,0:T(8,128)} %rows_ref.1, s32[4,1,32]{2,1,0:T(1,128)} %len_ref.1, s32[4,4,4]{2,1,0:T(4,128)} %src_ref.1, s32[4,4]{1,0:T(4,128)} %cnt_ref.1, bf16[4,4,4,128,128]{4,3,2,1,0:T(8,128)(2,1)} %tv_hbm.1, ...), custom_call_target="tpu_custom_call" | custom-call | tf_op jit(solution)/shard_map/pallas_call | solution.py:496
  151.0 3.0 %copy.12 = bf16[1,4,512,512]{3,2,1,0:T(8,128)(2,1)} copy(bf16[1,4,512,512]{3,2,1,0:T(8,128)(2,1)} %shard_map.100) | data formatting | bytes 4194304

commit v4 on v3

--- a/solution.py
+++ b/solution.py
@@ -19,6 +19,8 @@
 NH = 2
 HR = ROWS // NH
 BL = 4 // NH
+OH = 2
+OR = ROWS // OH
 
 
 def kernel(
@@ -129,48 +131,38 @@
             part = feat[h * HR:(h + 1) * HR, b * TILE:(b + 1) * TILE]
             xt[0, h, b * TILE:(b + 1) * TILE, :] = part.astype(F32).T.astype(BF16)
 
-    def t1_copy(l, h, o, c):
+    def t1_copy(l, h, c):
         return rcopy(
-            xt.at[l, h, pl.ds(pl.multiple_of(c * FS, FS), FS)], xc.at[l, h, k, r],
-            t1_s.at[l, h, o], t1_r.at[l, h, o], chip(c),
+            xt.at[l, h, pl.ds(pl.multiple_of(c * FS, FS), FS)], xc.at[l, h, k, r], t1_s.at[l, h], t1_r.at[l, h], chip(c)
         )
 
-    def t1_in(l, h, o):
-        ref = xc.at[l, h, k, fro(o)]
-        return rcopy(ref, ref, t1_s.at[l, h, o], t1_r.at[l, h, o], partner)
-
-    def row_of(dy):
-        return lax.rem(y + RING - dy, RING)
-
-    def fw_copy(l, h, dy, kk):
-        ref = xc.at[l, h, kk, pl.ds(row_of(dy) * RING, RING)]
-        return rcopy(ref, ref, fw_s.at[l, h, dy], fw_r.at[l, h, dy], partner)
+    def t1_all(l, h):
+        ref = xc.at[l, h, k, pl.ds(0, CHIPS - 1)]
+        return rcopy(ref, ref, t1_s.at[l, h], t1_r.at[l, h], partner)
+
+    def fw_copy(l, h, kk):
+        ref = xc.at[l, h, kk]
+        return rcopy(ref, ref, fw_s.at[l, h], fw_r.at[l, h], partner)
 
     def t1_start(l, h):
-        each(1, CHIPS, lambda o: t1_copy(l, h, o, to(o)).start())
+        each(1, CHIPS, lambda o: t1_copy(l, h, to(CHIPS - o)).start())
         xc[l, h, k, r] = xt[l, h, pl.ds(pl.multiple_of(r * FS, FS), FS), :]
 
-    def widen(l, h, dy, kk):
-        def one(e):
-            c = row_of(dy) * RING + e
-            xf[kk * CHIPS + c, :, h * HR:(h + 1) * HR] = xc[l, h, kk, c].astype(F32)
-        each(0, RING, one)
+    def widen(l, h, kk):
+        def four(g):
+            for e in range(RING):
+                c = g * RING + e
+                xf[kk * CHIPS + c, :, h * HR:(h + 1) * HR] = xc[l, h, kk, c].astype(F32)
+        each(0, CHIPS // RING, four)
 
     def t1_finish(l):
         for h in range(NH):
-            def arrive(dy):
-                @pl.when(dy > 0)
-                def _():
-                    t1_in(l, h, dy * RING).wait_recv()
-                each(1, RING, lambda dz: t1_in(l, h, dy * RING + dz).wait_recv())
-                fw_copy(l, h, dy, k).start()
-                widen(l, h, dy, k)
-            each(0, RING, arrive)
+            t1_all(l, h).wait_recv()
+            fw_copy(l, h, k).start()
+            widen(l, h, k)
         for h in range(NH):
-            def other(dy):
-                fw_copy(l, h, dy, 1 - k).wait_recv()
-                widen(l, h, dy, 1 - k)
-            each(0, RING, other)
+            fw_copy(l, h, 1 - k).wait_recv()
+            widen(l, h, 1 - k)
 
     for h in range(NH):
         t1_start(0, h)
@@ -238,7 +230,11 @@
 
     def t2_copy(l, h, o):
         c = to(o)
-        return rcopy(aggs.at[l, h, c], agg.at[l, h, r], t2_s.at[l, h, o], t2_r.at[l, h, o], chip(c))
+        return rcopy(aggs.at[l, h, c], agg.at[l, h, r], t2_s.at[l, h], t2_r.at[l, h], chip(c))
+
+    def t2_all(l, h):
+        ref = agg.at[l, h, pl.ds(0, CHIPS - 1)]
+        return rcopy(ref, ref, t2_s.at[l, h], t2_r.at[l, h], partner)
 
     def gather(o, blocks, buf):
         c = to(o)
@@ -258,25 +254,25 @@
 
     def aggregate(l, h):
         blocks = range(h * BL, (h + 1) * BL)
-        gather(1, blocks, ga)
+        gather(CHIPS - 1, blocks, ga)
 
         def two(t):
-            o = 2 * t + 1
+            o = CHIPS - 1 - 2 * t
             multiply(l, o, blocks, ga, aggs)
-            gather(o + 1, blocks, gb)
+            gather(o - 1, blocks, gb)
             t2_copy(l, h, o).start()
-            multiply(l, o + 1, blocks, gb, aggs)
-            gather(o + 2, blocks, ga)
-            t2_copy(l, h, o + 1).start()
+            multiply(l, o - 1, blocks, gb, aggs)
+            gather(o - 2, blocks, ga)
+            t2_copy(l, h, o - 1).start()
 
         each(0, CHIPS // 2 - 1, two)
-        multiply(l, CHIPS - 1, blocks, ga, aggs)
+        multiply(l, 1, blocks, ga, aggs)
         gather(0, blocks, gb)
-        t2_copy(l, h, CHIPS - 1).start()
+        t2_copy(l, h, 1).start()
         multiply(l, 0, blocks, gb, agg)
 
     def out_rows(l, h):
-        return outr.at[l, pl.ds(h * HR, HR)], out_hbm.at[0, x, pl.ds(h * HR, HR)]
+        return outr.at[l, pl.ds(h * OR, OR)], out_hbm.at[0, x, pl.ds(h * OR, OR)]
 
     def out_local(l, h):
         src, dst = out_rows(l, h)
@@ -289,38 +285,41 @@
 
     last = LAYERS - 1
 
-    def relay_in(h):
-        return rcopy(
-            outr.at[last, pl.ds(h * HR, HR)], relay, rl_s.at[h], rl_r, {"segment": last - 1 if h == 0 else 0}
-        )
-
-    def relay_out(h):
-        return rcopy(relay, out_hbm.at[0, 1, pl.ds(h * HR, HR)], rl_s.at[NH], o_r.at[2, h], {"segment": last})
+    def relay_in(e):
+        src, _ = out_rows(last, e)
+        return rcopy(src, relay, rl_s.at[e], rl_r, {"segment": last - 1 if e == 0 else 0})
+
+    def relay_out(e):
+        return rcopy(relay, out_hbm.at[0, 1, pl.ds(e * OR, OR)], rl_s.at[e], o_r.at[2, e], {"segment": last})
+
+    def by_place(l, local, remote, relayed):
+        far = (x == 1) & (l == last)
+        pl.when(x == l)(local)
+        pl.when((x != l) & jnp.logical_not(far))(remote)
+        pl.when(far)(relayed)
 
     def send_out(l, h):
         for b in range(D // TILE):
             part = xt[l + 1, h, b * TILE:(b + 1) * TILE, :]
             outr[l, h * HR:(h + 1) * HR, b * TILE:(b + 1) * TILE] = part.astype(F32).T.astype(BF16)
-
-        @pl.when(x == l)
-        def _():
-            out_local(l, h).start()
-
-        far = (x == 1) & (l == last)
-
-        @pl.when((x != l) & jnp.logical_not(far))
-        def _():
-            out_remote(l, h).start()
-
-        @pl.when(far)
-        def _():
-            relay_in(h).start()
+        halves = range(h * OH // NH, (h + 1) * OH // NH)
+
+        def local():
+            for e in halves:
+                out_local(l, e).start()
+
+        def remote():
+            for e in halves:
+                out_remote(l, e).start()
+
+        def relayed():
+            for e in halves:
+                relay_in(e).start()
+
+        by_place(l, local, remote, relayed)
 
     def dense(l, h):
-        def got(o):
-            ref = agg.at[l, h, fro(o)]
-            rcopy(ref, ref, t2_s.at[l, h, o], t2_r.at[l, h, o], partner).wait_recv()
-        each(1, CHIPS, got)
+        t2_all(l, h).wait_recv()
         rhs = agg[l, h].reshape(D, HR)
         v = pre[h] + jnp.dot(wp[l, :, D:2 * D], rhs, preferred_element_type=F32)
         pre[h] = v - jnp.mean(v, axis=0, keepdims=True)
@@ -334,10 +333,19 @@
             xt[l + 1, h, :, cols] = jnp.maximum(w, 0.0).astype(BF16)
 
     def advance(l, h):
-        @pl.when(l < LAYERS - 1)
+        @pl.when(l < last)
         def _():
             t1_start(l + 1, h)
-        send_out(l, h)
+
+        @pl.when(l == last)
+        def _():
+            send_out(l, h)
+
+        if h == NH - 1:
+            @pl.when(l < last)
+            def _():
+                for e in range(NH):
+                    send_out(l, e)
 
     for h in range(2):
         for s in (1, -1):
@@ -444,12 +452,12 @@
 
     each(1, LAYERS, layer)
 
-    for h, at_x in ((0, last - 1), (1, 0)):
+    for e, at_x in ((0, last - 1), (1, 0)):
         @pl.when(x == at_x)
         def _():
-            relay_in(h).wait_recv()
-            relay_out(h).start()
-            relay_out(h).wait_send()
+            relay_in(e).wait_recv()
+            relay_out(e).start()
+            relay_out(e).wait_send()
 
     for dct in (s1, s1b, s2, s2b):
         for c, _ in dct.values():
@@ -462,32 +470,30 @@
 
     def sent(l):
         for h in range(NH):
-            def one(o):
-                t1_copy(l, h, o, to(o)).wait_send()
-                t2_copy(l, h, o).wait_send()
-            each(1, CHIPS, one)
-            each(0, RING, lambda dy: fw_copy(l, h, dy, k).wait_send())
-
-            @pl.when(x == l)
-            def _():
-                out_local(l, h).wait()
-
-            far = (x == 1) & (l == last)
-
-            @pl.when((x != l) & jnp.logical_not(far))
-            def _():
-                out_remote(l, h).wait_send()
-
-            @pl.when(far)
-            def _():
-                relay_in(h).wait_send()
+            t1_all(l, h).wait_send()
+            t2_all(l, h).wait_send()
+            fw_copy(l, h, k).wait_send()
+
+        def local():
+            for e in range(OH):
+                out_local(l, e).wait()
+
+        def remote():
+            for e in range(OH):
+                out_remote(l, e).wait_send()
+
+        def relayed():
+            for e in range(OH):
+                relay_in(e).wait_send()
+
+        by_place(l, local, remote, relayed)
 
     each(0, LAYERS, sent)
     for j in range(1, LAYERS):
         c = lax.rem(x + j, LAYERS)
-        for h in range(NH):
-            src, _ = out_rows(0, h)
-            rcopy(src, out_hbm.at[0, c, pl.ds(h * HR, HR)], o_s.at[0, h], o_r.at[j, h], partner).wait_recv()
+        for e in range(OH):
+            src, _ = out_rows(0, e)
+            rcopy(src, out_hbm.at[0, c, pl.ds(e * OR, OR)], o_s.at[0, e], o_r.at[j, e], partner).wait_recv()
 
 
 def per_device(features, send_rows, send_len, tile_src, tile_count, tile_val, w_self, w_neigh, gain, bias):
@@ -503,7 +509,7 @@
             pltpu.VMEM((4, 4, TILE, TILE), BF16),
             pltpu.VMEM((FS, 16 * TILE), BF16),
             pltpu.VMEM((FS, 16 * TILE), BF16),
-            pltpu.VMEM((HR, D), BF16),
+            pltpu.VMEM((OR, D), BF16),
             pltpu.VMEM((LAYERS + 1, NH, D, HR), BF16),
             pltpu.VMEM((LAYERS, D, 2 * D + 2 * AUX), BF16),
             pltpu.VMEM((CHIPS, 4, 4, TILE, TILE), BF16),
@@ -519,14 +525,14 @@
             pltpu.VMEM((LAYERS, ROWS, D), BF16),
             pltpu.VMEM((NH, D, HR), F32),
             pltpu.SMEM((CHIPS, 8, TILE), I32),
-            dma((3,)), dma((NH,)), dma((NH + 1,)), dma,
+            dma((3,)), dma((OH,)), dma((OH,)), dma,
             dma((48,)), dma((48,)),
-            dma((LAYERS, NH, CHIPS)), dma((LAYERS, NH, CHIPS)),
-            dma((LAYERS, NH, RING)), dma((LAYERS, NH, RING)),
-            dma((LAYERS, NH, CHIPS)), dma((LAYERS, NH, CHIPS)),
+            dma((LAYERS, NH)), dma((LAYERS, NH)),
+            dma((LAYERS, NH)), dma((LAYERS, NH)),
+            dma((LAYERS, NH)), dma((LAYERS, NH)),
             dma((LAYERS,)), dma((LAYERS,)),
             dma((LAYERS,)), dma((LAYERS,)),
-            dma((LAYERS, NH)), dma((LAYERS, NH)),
+            dma((LAYERS, OH)), dma((LAYERS, OH)),
             dma((CHIPS,)), dma((CHIPS,)),
             dma((CHIPS,)), dma((CHIPS,)),
             dma, dma,

time: 154 us -> 150 us (0.974)
  Pallas kernels: 151 us -> 147 us
    pallas_call x1, Pallas kernels: 151 us -> 147 us  [per_device(): pl.pallas_call(kernel, out_shape=jax.ShapeDtypeStruct((1, 4, ROWS, D), BF...]
where the time goes in v4:
time: 150 us
  Pallas kernels  147 us (98%)
  local copies, waits for them, and re-layouts  3.05 us (2%)
    pallas_call x1, Pallas kernels, per_device(): pl.pallas_call(kernel, out_shape=jax.ShapeDtypeStruct((1, 4, ROWS, D), BF...  147 us
    unnamed x1, local copies, waits for them, and re-layouts  3.05 us

profile of v4, /device:TPU:6, one launch (start us, length us, event | category | flops | bytes accessed | tf_op | source)
XLA Modules:
  0.0 150.2 jit_solution(13026513877270843324)
XLA Ops:
  0.0 147.2 %shard_map.100 = bf16[1,4,512,512]{3,2,1,0:T(8,128)(2,1)} custom-call(bf16[4,512,512]{2,1,0:T(8,128)(2,1)} %feat_hbm.1, s32[4,1,32,128]{3,2,1,0:T(8,128)} %rows_ref.1, s32[4,1,32]{2,1,0:T(1,128)} %len_ref.1, s32[4,4,4]{2,1,0:T(4,128)} %src_ref.1, s32[4,4]{1,0:T(4,128)} %cnt_ref.1, bf16[4,4,4,128,128]{4,3,2,1,0:T(8,128)(2,1)} %tv_hbm.1, ...), custom_call_target="tpu_custom_call" | custom-call | tf_op jit(solution)/shard_map/pallas_call | solution.py:502
  147.2 3.0 %copy.12 = bf16[1,4,512,512]{3,2,1,0:T(8,128)(2,1)} copy(bf16[1,4,512,512]{3,2,1,0:T(8,128)(2,1)} %shard_map.100) | data formatting | bytes 4194304

commit v5 on v4

--- a/solution.py
+++ b/solution.py
@@ -35,6 +35,9 @@
     r = lax.div(d, 2)
     y, z = lax.div(r, RING), lax.rem(r, RING)
 
+    def at_offset(dy, dz):
+        return lax.rem(y + dy, RING) * RING + lax.rem(z + dz, RING)
+
     def to(o):
         return lax.rem(y + lax.div(o, RING), RING) * RING + lax.rem(z + lax.rem(o, RING), RING)
 
@@ -145,7 +148,10 @@
         return rcopy(ref, ref, fw_s.at[l, h], fw_r.at[l, h], partner)
 
     def t1_start(l, h):
-        each(1, CHIPS, lambda o: t1_copy(l, h, to(CHIPS - o)).start())
+        for dy in (2, 3, 1, 0):
+            for dz in (2, 3, 1, 0):
+                if dy or dz:
+                    t1_copy(l, h, at_offset(dy, dz)).start()
         xc[l, h, k, r] = xt[l, h, pl.ds(pl.multiple_of(r * FS, FS), FS), :]
 
     def widen(l, h, kk):
@@ -228,23 +234,20 @@
             g = jnp.where(high == b, part, g)
         return g.astype(BF16)
 
-    def t2_copy(l, h, o):
-        c = to(o)
+    def t2_copy(l, h, c):
         return rcopy(aggs.at[l, h, c], agg.at[l, h, r], t2_s.at[l, h], t2_r.at[l, h], chip(c))
 
     def t2_all(l, h):
         ref = agg.at[l, h, pl.ds(0, CHIPS - 1)]
         return rcopy(ref, ref, t2_s.at[l, h], t2_r.at[l, h], partner)
 
-    def gather(o, blocks, buf):
-        c = to(o)
+    def gather(c, blocks, buf):
         for b, i in enumerate(blocks):
             for kk in range(4):
                 t = 4 * i + kk
                 buf[:, (4 * b + kk) * TILE:(4 * b + kk + 1) * TILE] = gathered(qs[c, 0, t], meta[c, t:t + 1, :])
 
-    def multiply(l, o, blocks, buf, dst):
-        c = to(o)
+    def multiply(l, c, blocks, buf, dst):
         for b, i in enumerate(blocks):
             a = jnp.dot(
                 buf[:, 4 * b * TILE:4 * (b + 1) * TILE], tv[c, i].reshape(4 * TILE, TILE), preferred_element_type=F32
@@ -254,22 +257,24 @@
 
     def aggregate(l, h):
         blocks = range(h * BL, (h + 1) * BL)
-        gather(CHIPS - 1, blocks, ga)
-
-        def two(t):
-            o = CHIPS - 1 - 2 * t
-            multiply(l, o, blocks, ga, aggs)
-            gather(o - 1, blocks, gb)
-            t2_copy(l, h, o).start()
-            multiply(l, o - 1, blocks, gb, aggs)
-            gather(o - 2, blocks, ga)
-            t2_copy(l, h, o - 1).start()
-
-        each(0, CHIPS // 2 - 1, two)
-        multiply(l, 1, blocks, ga, aggs)
-        gather(0, blocks, gb)
-        t2_copy(l, h, 1).start()
-        multiply(l, 0, blocks, gb, agg)
+        bufs = (ga, gb)
+        gather(at_offset(RING - 1, RING - 1), blocks, ga)
+
+        def row(dy, own):
+            for n in range(RING):
+                dz = RING - 1 - n
+                c = at_offset(dy, dz)
+                mine = own and dz == 0
+                multiply(l, c, blocks, bufs[n % 2], agg if mine else aggs)
+                if dz:
+                    gather(at_offset(dy, dz - 1), blocks, bufs[(n + 1) % 2])
+                elif not own:
+                    gather(at_offset(dy - 1, RING - 1), blocks, ga)
+                if not mine:
+                    t2_copy(l, h, c).start()
+
+        each(0, RING - 1, lambda t: row(RING - 1 - t, False))
+        row(0, True)
 
     def out_rows(l, h):
         return outr.at[l, pl.ds(h * OR, OR)], out_hbm.at[0, x, pl.ds(h * OR, OR)]
@@ -381,6 +386,9 @@
         for s in (1, -1):
             ring_wait(s1b[h, s], True, s)
         second(h, 2)
+    for da in (1, -1):
+        for h in range(2):
+            second_fwd(h, da)
 
     t1_finish(0)
     each(1, CHIPS, lambda o: meta_copy(o, fro(o), partner).wait_recv())
@@ -396,34 +404,31 @@
         (0, 0), (0, 1), (0, -1), (1, 0), (-1, 0), (0, 2), (2, 0), (1, 1), (-1, -1), (1, -1), (-1, 1),
         (2, 1), (2, -1), (1, 2), (-1, 2), (2, 2),
     ]
-    offsets = [dy % RING * RING + dz % RING for dy, dz in order]
+    offsets = [(dy % RING, dz % RING) for dy, dz in order]
     bufs = (ga, gb)
-    gather(offsets[0], range(4), ga)
+    gather(at_offset(*offsets[0]), range(4), ga)
 
     def first_layer(lo, hi):
         for u in range(lo, hi):
-            o = offsets[u]
-            multiply(0, o, range(4), bufs[u % 2], aggs if o else agg)
+            c = at_offset(*offsets[u])
+            multiply(0, c, range(4), bufs[u % 2], aggs if u else agg)
             if u + 1 < CHIPS:
-                gather(offsets[u + 1], range(4), bufs[(u + 1) % 2])
-            if o:
+                gather(at_offset(*offsets[u + 1]), range(4), bufs[(u + 1) % 2])
+            if u:
                 for h in range(NH):
-                    t2_copy(0, h, o).start()
+                    t2_copy(0, h, c).start()
 
     first_layer(0, 5)
-    for da in (1, -1):
-        for h in range(2):
-            second_fwd(h, da)
+    for h in range(2):
+        second_fwd(h, 2)
     arrived([(h, 0, s) for h in range(2) for s in (1, -1)])
     first_layer(5, 11)
-    for h in range(2):
-        second_fwd(h, 2)
+    for j in range(1, LAYERS):
+        w_forward(j)
     arrived([(h, da, s) for da in (1, -1) for h in range(2) for s in (1, -1)])
     first_layer(11, 15)
     arrived([(h, 2, s) for h in range(2) for s in (1, -1)])
     first_layer(15, 16)
-    for j in range(1, LAYERS):
-        w_forward(j)
 
     def own_part(l):
         @pl.when(x != l)

time: 150 us -> 148 us (0.987)
  Pallas kernels: 147 us -> 145 us
    pallas_call x1, Pallas kernels: 147 us -> 145 us  [per_device(): pl.pallas_call(kernel, out_shape=jax.ShapeDtypeStruct((1, 4, ROWS, D), BF...]
where the time goes in v5:
time: 148 us
  Pallas kernels  145 us (98%)
  local copies, waits for them, and re-layouts  3.05 us (2%)
    pallas_call x1, Pallas kernels, per_device(): pl.pallas_call(kernel, out_shape=jax.ShapeDtypeStruct((1, 4, ROWS, D), BF...  145 us
    unnamed x1, local copies, waits for them, and re-layouts  3.05 us

profile of v5, /device:TPU:6, one launch (start us, length us, event | category | flops | bytes accessed | tf_op | source)
XLA Modules:
  0.0 148.1 jit_solution(13310502569214588967)
XLA Ops:
  0.0 145.1 %shard_map.100 = bf16[1,4,512,512]{3,2,1,0:T(8,128)(2,1)} custom-call(bf16[4,512,512]{2,1,0:T(8,128)(2,1)} %feat_hbm.1, s32[4,1,32,128]{3,2,1,0:T(8,128)} %rows_ref.1, s32[4,1,32]{2,1,0:T(1,128)} %len_ref.1, s32[4,4,4]{2,1,0:T(4,128)} %src_ref.1, s32[4,4]{1,0:T(4,128)} %cnt_ref.1, bf16[4,4,4,128,128]{4,3,2,1,0:T(8,128)(2,1)} %tv_hbm.1, ...), custom_call_target="tpu_custom_call" | custom-call | tf_op jit(solution)/shard_map/pallas_call | solution.py:507
  145.1 3.0 %copy.12 = bf16[1,4,512,512]{3,2,1,0:T(8,128)(2,1)} copy(bf16[1,4,512,512]{3,2,1,0:T(8,128)(2,1)} %shard_map.100) | data formatting | bytes 4194304

commit v6 on v5

--- a/solution.py
+++ b/solution.py
@@ -24,10 +24,10 @@
 
 
 def kernel(
-    feat_hbm, rows_ref, len_ref, src_ref, cnt_ref, tv_hbm, ws_ref, wn_ref, gain_ref, bias_ref,
+    feat_hbm, rows_ref, len_ref, src_ref, cnt_ref, tv_hbm, ws_hbm, wn_hbm, gain_ref, bias_ref,
     out_hbm,
-    feat, tvs, ga, gb, relay, xt, wp, tv, meta, m1a, px, m1b, m1c, xc, xf, aggs, agg, outr, pre, qs,
-    loc_sem, ol_sem, rl_s, rl_r, tv_s, tv_r, t1_s, t1_r, fw_s, fw_r, t2_s, t2_r, w_s, w_r, wf_s, wf_r, o_s, o_r, m_s, m_r, mb_s, mb_r, pm_s, pm_r,
+    feat, tvs, w_in, ga, gb, relay, xt, wp, tv, meta, m1a, px, m1b, m1c, xc, xf, aggs, agg, outr, pre, qs,
+    loc_sem, ol_sem, rl_s, rl_r, ro_s, tv_s, tv_r, t1_s, t1_r, fw_s, fw_r, t2_s, t2_r, w_s, w_r, wf_s, wf_r, o_s, o_r, m_s, m_r, mb_s, mb_r, pm_s, pm_r,
 ):
     x = lax.axis_index("segment")
     d = lax.axis_index("dom")
@@ -68,8 +68,11 @@
 
     load_f = pltpu.make_async_copy(feat_hbm.at[x], feat, loc_sem.at[0])
     load_t = pltpu.make_async_copy(tv_hbm.at[x], tvs, loc_sem.at[1])
+    load_w = [pltpu.make_async_copy(src.at[0], w_in.at[e], loc_sem.at[3 + e]) for e, src in enumerate((ws_hbm, wn_hbm))]
+    load_t.start()
     load_f.start()
-    load_t.start()
+    for copy in load_w:
+        copy.start()
 
     barrier = pltpu.get_barrier_semaphore()
     each(1, CHIPS, lambda o: pl.semaphore_signal(barrier, inc=1, device_id=chip(to(o)), device_id_type=MESH))
@@ -182,10 +185,12 @@
     pm = rcopy(m1a.at[1 - k], px, pm_s, pm_r, partner)
     pm.start()
 
+    for copy in load_w:
+        copy.wait()
     for b in range(D // TILE):
         cols = slice(b * TILE, (b + 1) * TILE)
-        wp[x, cols, 0:D] = ws_ref[0, :, cols].astype(F32).T.astype(BF16)
-        wp[x, cols, D:2 * D] = wn_ref[0, :, cols].astype(F32).T.astype(BF16)
+        wp[x, cols, 0:D] = w_in[0, :, cols].astype(F32).T.astype(BF16)
+        wp[x, cols, D:2 * D] = w_in[1, :, cols].astype(F32).T.astype(BF16)
         wp[x, cols, 2 * D:2 * D + AUX] = jnp.broadcast_to(gain_ref[:, cols].astype(F32), (AUX, TILE)).T.astype(BF16)
         wp[x, cols, 2 * D + AUX:2 * D + 2 * AUX] = (
             jnp.broadcast_to(bias_ref[:, cols].astype(F32), (AUX, TILE)).T.astype(BF16)
@@ -290,15 +295,26 @@
 
     last = LAYERS - 1
 
-    def relay_in(e):
-        src, _ = out_rows(last, e)
-        return rcopy(src, relay, rl_s.at[e], rl_r, {"segment": last - 1 if e == 0 else 0})
-
-    def relay_out(e):
-        return rcopy(relay, out_hbm.at[0, 1, pl.ds(e * OR, OR)], rl_s.at[e], o_r.at[2, e], {"segment": last})
+    def relay_in(l, e):
+        src, _ = out_rows(l, e)
+        via = lax.rem(l + (LAYERS - 1 if e == 0 else 1), LAYERS)
+        return rcopy(src, relay, rl_s.at[e], rl_r, {"segment": via})
+
+    def relay_out(l, e):
+        return rcopy(relay, out_hbm.at[0, l - 2, pl.ds(e * OR, OR)], ro_s, o_r.at[2, e], {"segment": l})
+
+    def pass_on(l, finish):
+        for e, at_x in ((0, (l + 3) % LAYERS), (1, (l + 1) % LAYERS)):
+            @pl.when(x == at_x)
+            def _():
+                if finish:
+                    relay_out(l, e).wait_send()
+                else:
+                    relay_in(l, e).wait_recv()
+                    relay_out(l, e).start()
 
     def by_place(l, local, remote, relayed):
-        far = (x == 1) & (l == last)
+        far = x == l - 2
         pl.when(x == l)(local)
         pl.when((x != l) & jnp.logical_not(far))(remote)
         pl.when(far)(relayed)
@@ -319,7 +335,7 @@
 
         def relayed():
             for e in halves:
-                relay_in(e).start()
+                relay_in(l, e).start()
 
         by_place(l, local, remote, relayed)
 
@@ -447,6 +463,7 @@
     def layer(l):
         own_part(l)
         t1_finish(l)
+        pl.when(l == last)(lambda: pass_on(last - 1, False))
         for h in range(NH):
             aggregate(l, h)
             if h > 0:
@@ -457,12 +474,7 @@
 
     each(1, LAYERS, layer)
 
-    for e, at_x in ((0, last - 1), (1, 0)):
-        @pl.when(x == at_x)
-        def _():
-            relay_in(e).wait_recv()
-            relay_out(e).start()
-            relay_out(e).wait_send()
+    pass_on(last, False)
 
     for dct in (s1, s1b, s2, s2b):
         for c, _ in dct.values():
@@ -489,11 +501,13 @@
 
         def relayed():
             for e in range(OH):
-                relay_in(e).wait_send()
+                relay_in(l, e).wait_send()
 
         by_place(l, local, remote, relayed)
 
     each(0, LAYERS, sent)
+    pass_on(last - 1, True)
+    pass_on(last, True)
     for j in range(1, LAYERS):
         c = lax.rem(x + j, LAYERS)
         for e in range(OH):
@@ -507,11 +521,12 @@
     return pl.pallas_call(
         kernel,
         out_shape=jax.ShapeDtypeStruct((1, 4, ROWS, D), BF16),
-        in_specs=[any_, vmem, smem, smem, smem, any_, vmem, vmem, vmem, vmem],
+        in_specs=[any_, vmem, smem, smem, smem, any_, any_, any_, vmem, vmem],
         out_specs=any_,
         scratch_shapes=[
             pltpu.VMEM((ROWS, D), BF16),
             pltpu.VMEM((4, 4, TILE, TILE), BF16),
+            pltpu.VMEM((2, D, D), BF16),
             pltpu.VMEM((FS, 16 * TILE), BF16),
             pltpu.VMEM((FS, 16 * TILE), BF16),
             pltpu.VMEM((OR, D), BF16),
@@ -530,7 +545,7 @@
             pltpu.VMEM((LAYERS, ROWS, D), BF16),
             pltpu.VMEM((NH, D, HR), F32),
             pltpu.SMEM((CHIPS, 8, TILE), I32),
-            dma((3,)), dma((OH,)), dma((OH,)), dma,
+            dma((5,)), dma((OH,)), dma((OH,)), dma, dma,
             dma((48,)), dma((48,)),
             dma((LAYERS, NH)), dma((LAYERS, NH)),
             dma((LAYERS, NH)), dma((LAYERS, NH)),

time: 148 us -> 146 us (0.986)
  Pallas kernels: 145 us -> 143 us
    pallas_call x1, Pallas kernels: 145 us -> 143 us  [per_device(): pl.pallas_call(kernel, out_shape=jax.ShapeDtypeStruct((1, 4, ROWS, D), BF...]
where the time goes in v6:
time: 146 us
  Pallas kernels  143 us (98%)
  local copies, waits for them, and re-layouts  3.05 us (2%)
    pallas_call x1, Pallas kernels, per_device(): pl.pallas_call(kernel, out_shape=jax.ShapeDtypeStruct((1, 4, ROWS, D), BF...  143 us
    unnamed x1, local copies, waits for them, and re-layouts  3.05 us

profile of v6, /device:TPU:6, one launch (start us, length us, event | category | flops | bytes accessed | tf_op | source)
XLA Modules:
  0.0 146.2 jit_solution(4369413076744094910)
XLA Ops:
  0.0 143.1 %shard_map.100 = bf16[1,4,512,512]{3,2,1,0:T(8,128)(2,1)} custom-call(bf16[4,512,512]{2,1,0:T(8,128)(2,1)} %feat_hbm.1, s32[4,1,32,128]{3,2,1,0:T(8,128)} %rows_ref.1, s32[4,1,32]{2,1,0:T(1,128)} %len_ref.1, s32[4,4,4]{2,1,0:T(4,128)} %src_ref.1, s32[4,4]{1,0:T(4,128)} %cnt_ref.1, bf16[4,4,4,128,128]{4,3,2,1,0:T(8,128)(2,1)} %tv_hbm.1, ...), custom_call_target="tpu_custom_call" | custom-call | tf_op jit(solution)/shard_map/pallas_call | solution.py:521
  143.1 3.0 %copy.12 = bf16[1,4,512,512]{3,2,1,0:T(8,128)(2,1)} copy(bf16[1,4,512,512]{3,2,1,0:T(8,128)(2,1)} %shard_map.100) | data formatting | bytes 4194304

commit v7 on v6

--- a/solution.py
+++ b/solution.py
@@ -11,6 +11,7 @@
 LAYERS = 4
 RING = 4
 CHIPS = 16
+GROUP = CHIPS // 2
 TILE = 128
 ROWS = 512
 D = 512
@@ -137,41 +138,44 @@
             part = feat[h * HR:(h + 1) * HR, b * TILE:(b + 1) * TILE]
             xt[0, h, b * TILE:(b + 1) * TILE, :] = part.astype(F32).T.astype(BF16)
 
-    def t1_copy(l, h, c):
+    def t1_copy(l, h, dy, dz):
+        c, g = at_offset(dy, dz), dy // 2
         return rcopy(
-            xt.at[l, h, pl.ds(pl.multiple_of(c * FS, FS), FS)], xc.at[l, h, k, r], t1_s.at[l, h], t1_r.at[l, h], chip(c)
+            xt.at[l, h, pl.ds(pl.multiple_of(c * FS, FS), FS)], xc.at[l, h, k, dy * RING + dz],
+            t1_s.at[l, h, g], t1_r.at[l, h, g], chip(c),
         )
 
-    def t1_all(l, h):
-        ref = xc.at[l, h, k, pl.ds(0, CHIPS - 1)]
-        return rcopy(ref, ref, t1_s.at[l, h], t1_r.at[l, h], partner)
-
-    def fw_copy(l, h, kk):
-        ref = xc.at[l, h, kk]
-        return rcopy(ref, ref, fw_s.at[l, h], fw_r.at[l, h], partner)
+    def t1_all(l, h, g):
+        lo = max(g * GROUP, 1)
+        ref = xc.at[l, h, k, pl.ds(lo, (g + 1) * GROUP - lo)]
+        return rcopy(ref, ref, t1_s.at[l, h, g], t1_r.at[l, h, g], partner)
+
+    def fw_copy(l, h, g, kk):
+        ref = xc.at[l, h, kk, pl.ds(g * GROUP, GROUP)]
+        return rcopy(ref, ref, fw_s.at[l, h, g], fw_r.at[l, h, g], partner)
 
     def t1_start(l, h):
         for dy in (2, 3, 1, 0):
             for dz in (2, 3, 1, 0):
                 if dy or dz:
-                    t1_copy(l, h, at_offset(dy, dz)).start()
-        xc[l, h, k, r] = xt[l, h, pl.ds(pl.multiple_of(r * FS, FS), FS), :]
-
-    def widen(l, h, kk):
-        def four(g):
-            for e in range(RING):
-                c = g * RING + e
-                xf[kk * CHIPS + c, :, h * HR:(h + 1) * HR] = xc[l, h, kk, c].astype(F32)
-        each(0, CHIPS // RING, four)
+                    t1_copy(l, h, dy, dz).start()
+        xc[l, h, k, 0] = xt[l, h, pl.ds(pl.multiple_of(r * FS, FS), FS), :]
+
+    def widen(l, h, g, kk):
+        for o in range(g * GROUP, (g + 1) * GROUP):
+            c = at_offset(RING - o // RING, RING - o % RING)
+            xf[kk * CHIPS + c, :, h * HR:(h + 1) * HR] = xc[l, h, kk, o].astype(F32)
 
     def t1_finish(l):
         for h in range(NH):
-            t1_all(l, h).wait_recv()
-            fw_copy(l, h, k).start()
-            widen(l, h, k)
+            for g in range(2):
+                t1_all(l, h, g).wait_recv()
+                fw_copy(l, h, g, k).start()
+                widen(l, h, g, k)
         for h in range(NH):
-            fw_copy(l, h, 1 - k).wait_recv()
-            widen(l, h, 1 - k)
+            for g in range(2):
+                fw_copy(l, h, g, 1 - k).wait_recv()
+                widen(l, h, g, 1 - k)
 
     for h in range(NH):
         t1_start(0, h)
@@ -487,9 +491,10 @@
 
     def sent(l):
         for h in range(NH):
-            t1_all(l, h).wait_send()
             t2_all(l, h).wait_send()
-            fw_copy(l, h, k).wait_send()
+            for g in range(2):
+                t1_all(l, h, g).wait_send()
+                fw_copy(l, h, g, k).wait_send()
 
         def local():
             for e in range(OH):
@@ -547,8 +552,8 @@
             pltpu.SMEM((CHIPS, 8, TILE), I32),
             dma((5,)), dma((OH,)), dma((OH,)), dma, dma,
             dma((48,)), dma((48,)),
-            dma((LAYERS, NH)), dma((LAYERS, NH)),
-            dma((LAYERS, NH)), dma((LAYERS, NH)),
+            dma((LAYERS, NH, 2)), dma((LAYERS, NH, 2)),
+            dma((LAYERS, NH, 2)), dma((LAYERS, NH, 2)),
             dma((LAYERS, NH)), dma((LAYERS, NH)),
             dma((LAYERS,)), dma((LAYERS,)),
             dma((LAYERS,)), dma((LAYERS,)),

time: 146 us -> 147 us (level)
  no operation moved by 1% of the time
where the time goes in v7:
time: 147 us
  Pallas kernels  144 us (98%)
  local copies, waits for them, and re-layouts  3.05 us (2%)
    pallas_call x1, Pallas kernels, per_device(): pl.pallas_call(kernel, out_shape=jax.ShapeDtypeStruct((1, 4, ROWS, D), BF...  144 us
    unnamed x1, local copies, waits for them, and re-layouts  3.05 us

profile of v7, /device:TPU:6, one launch (start us, length us, event | category | flops | bytes accessed | tf_op | source)
XLA Modules:
  0.0 146.6 jit_solution(5231400652739093787)
XLA Ops:
  0.0 143.6 %shard_map.100 = bf16[1,4,512,512]{3,2,1,0:T(8,128)(2,1)} custom-call(bf16[4,512,512]{2,1,0:T(8,128)(2,1)} %feat_hbm.1, s32[4,1,32,128]{3,2,1,0:T(8,128)} %rows_ref.1, s32[4,1,32]{2,1,0:T(1,128)} %len_ref.1, s32[4,4,4]{2,1,0:T(4,128)} %src_ref.1, s32[4,4]{1,0:T(4,128)} %cnt_ref.1, bf16[4,4,4,128,128]{4,3,2,1,0:T(8,128)(2,1)} %tv_hbm.1, ...), custom_call_target="tpu_custom_call" | custom-call | tf_op jit(solution)/shard_map/pallas_call | solution.py:526
  143.6 3.0 %copy.12 = bf16[1,4,512,512]{3,2,1,0:T(8,128)(2,1)} copy(bf16[1,4,512,512]{3,2,1,0:T(8,128)(2,1)} %shard_map.100) | data formatting | bytes 4194304

commit v8 on v6

--- a/solution.py
+++ b/solution.py
@@ -169,7 +169,6 @@
             t1_all(l, h).wait_recv()
             fw_copy(l, h, k).start()
             widen(l, h, k)
-        for h in range(NH):
             fw_copy(l, h, 1 - k).wait_recv()
             widen(l, h, 1 - k)
 

time: 146 us -> 147 us (level)
  no operation moved by 1% of the time
where the time goes in v8:
time: 147 us
  Pallas kernels  144 us (98%)
  local copies, waits for them, and re-layouts  3.05 us (2%)
    pallas_call x1, Pallas kernels, per_device(): pl.pallas_call(kernel, out_shape=jax.ShapeDtypeStruct((1, 4, ROWS, D), BF...  144 us
    unnamed x1, local copies, waits for them, and re-layouts  3.05 us

profile of v8, /device:TPU:6, one launch (start us, length us, event | category | flops | bytes accessed | tf_op | source)
XLA Modules:
  0.0 146.8 jit_solution(18281112221529507484)
XLA Ops:
  0.0 143.7 %shard_map.100 = bf16[1,4,512,512]{3,2,1,0:T(8,128)(2,1)} custom-call(bf16[4,512,512]{2,1,0:T(8,128)(2,1)} %feat_hbm.1, s32[4,1,32,128]{3,2,1,0:T(8,128)} %rows_ref.1, s32[4,1,32]{2,1,0:T(1,128)} %len_ref.1, s32[4,4,4]{2,1,0:T(4,128)} %src_ref.1, s32[4,4]{1,0:T(4,128)} %cnt_ref.1, bf16[4,4,4,128,128]{4,3,2,1,0:T(8,128)(2,1)} %tv_hbm.1, ...), custom_call_target="tpu_custom_call" | custom-call | tf_op jit(solution)/shard_map/pallas_call | solution.py:520
  143.7 3.0 %copy.12 = bf16[1,4,512,512]{3,2,1,0:T(8,128)(2,1)} copy(bf16[1,4,512,512]{3,2,1,0:T(8,128)(2,1)} %shard_map.100) | data formatting | bytes 4194304
